TPU v7x, 512 devices: a whole 4x8x8 slice. The times are simulated.
512 devices in a mesh: dom: 8 (over y), dp: 64 (over z, x, core).
Axes of the slice: x: 4, y: 8, z: 8, core: 2. Of those that a mesh axis runs over, the one named last changes fastest.
Arguments:
- positions: float32 [512, 32768], P('dom', 'dp'), may hold values from -6 to 6
- ancestors: int32 [512], P('dom'), may hold values from 0 to 511
- block_choice: int32 [64, 64], replicated, may hold values from 0 to 3
- tile_slot: int32 [1024, 8], P('dp'), may hold values from 0 to 63, all different within a row
- design: bfloat16 [131072, 1024], P('dp'), may hold values from -0.1875 to 0.1875
- labels: int32 [131072], P('dp'), may hold values 0 or 1
- row_section: int32 [131072], P('dp'), may hold values from 0 to 4
Outputs:
- advanced: float32 [512, 32768], P('dom', 'dp')
- mean_loglik: float32 [512], P('dom')
Inputs may be any that keep to these rules, and one draw needn't show every extreme that they name: Each row of tile_slot names 8 different owners.
All inputs are finite; a program needn't handle non-finite values. No bound on the sum of `labels` on one device may be relied on, other than what follows from the above.
Results may differ from a plain program's by a relative error of at most 0.00048.
Values may be sent and summed in bfloat16 or wider, within the bound.
No kernel may reach another device: no remote copies, remote signals or barrier semaphores. Data moves between devices by JAX's collectives and lax.ppermute only.
A program may use at most 64 MiB of HBM per device.

v0:
```python
import jax
import jax.numpy as jnp
from jax import lax
from jax.sharding import PartitionSpec as P

TILE = 128
CURRENT = 2


step_size = 1.0
prior_precision = 0.05


def spread_blocks(source, block_choice, device_index, data_width):
    narrow = source.astype(jnp.bfloat16)
    particle_count = narrow.shape[0]
    blocks_owned = narrow.shape[1] // TILE
    gathered = lax.all_gather(narrow, "dp", axis=1, tiled=True)
    gathered = gathered.reshape(particle_count, data_width, blocks_owned, TILE)
    selection = lax.dynamic_index_in_dim(block_choice, device_index, 0, keepdims=False)
    return jnp.take_along_axis(gathered, selection[None, :, None, None], axis=2)[:, :, 0]


def tile_logits(fetched, design_tiles, tile_slot):
    weights = jnp.take(fetched, tile_slot, axis=1)
    return jnp.einsum("bikc,pbkc->bpi", design_tiles, weights, preferred_element_type=jnp.float32)


def shards(positions, ancestors, block_choice, tile_slot, design, labels, row_section):
    data_width = lax.axis_size("dp")
    device_index = lax.axis_index("dp")
    lineage = lax.all_gather(positions, "dom", axis=0, tiled=True)
    resampled = jnp.take(lineage, ancestors, axis=0)
    particle_count = resampled.shape[0]
    blocks_owned = positions.shape[1] // TILE
    blocks_dev = tile_slot.shape[0]
    per_block = tile_slot.shape[1]
    design_tiles = design.reshape(blocks_dev, TILE, per_block, TILE)
    targets = labels.reshape(blocks_dev, 1, TILE).astype(jnp.float32)
    sections = row_section.reshape(blocks_dev, 1, TILE)
    fetched = spread_blocks(resampled, block_choice, device_index, data_width)
    logits = tile_logits(fetched, design_tiles, tile_slot)
    residual = jnp.where(sections <= CURRENT, targets - jax.nn.sigmoid(logits), 0.0).astype(
        jnp.bfloat16
    )
    per_tile = jnp.einsum(
        "bpi,bikc->bkpc", residual, design_tiles, preferred_element_type=jnp.float32
    )
    flat_terms = per_tile.reshape(blocks_dev * per_block, particle_count * TILE)
    outgoing = jax.ops.segment_sum(flat_terms, tile_slot.reshape(-1), num_segments=data_width)
    outgoing = outgoing.reshape(data_width, particle_count, TILE)
    incoming = lax.all_to_all(outgoing, "dp", split_axis=0, concat_axis=0, tiled=True)
    column = lax.dynamic_index_in_dim(block_choice, device_index, 1, keepdims=False)
    owner_hot = (column[:, None] == jnp.arange(blocks_owned)[None, :]).astype(jnp.float32)
    gradient = jnp.einsum("spc,sq->pqc", incoming, owner_hot, precision=lax.Precision.HIGHEST)
    gradient = gradient.reshape(particle_count, blocks_owned * TILE)
    advanced = resampled + step_size * (gradient - prior_precision * resampled)
    fetched_new = spread_blocks(advanced, block_choice, device_index, data_width)
    logits_new = tile_logits(fetched_new, design_tiles, tile_slot)
    chosen = sections == CURRENT + 1
    loglik = jnp.where(chosen, targets * logits_new - jax.nn.softplus(logits_new), 0.0)
    totals = jnp.sum(loglik, axis=(0, 2))
    counted = jnp.sum(chosen.astype(jnp.float32))
    totals, counted = lax.psum((totals, counted), "dp")
    return (advanced, totals / jnp.maximum(counted, 1.0))


def solution(mesh):
    return jax.shard_map(
        shards,
        mesh=mesh,
        in_specs=(P("dom", "dp"), P("dom"), P(), P("dp", None), P("dp", None), P("dp"), P("dp")),
        out_specs=(P("dom", "dp"), P("dom")),
        check_vma=False,
    )
```

profile of v0, /device:TPU:1, one launch (start us, length us, event | category | flops | bytes accessed | tf_op | source)
XLA Modules:
  0.0 479.8 jit_solution(3717747859141420271)
XLA Ops:
  9.3 42.2 %all-gather.4.cloned.1.call-done = f32[512,512]{1,0:T(8,128)} async-done(((f32[64,512]{1,0:T(8,128)}), f32[512,512]{1,0:T(8,128)}) %all-gather.4.cloned.1.call-update) | async-done | bytes 1048592 | tf_op jit(solution)/shard_map/all_gather | solution.py:32
  51.5 1.9 gather_fusion
  53.4 0.7 select_convert_fusion
  54.2 0.8 copy.27
  55.1 5.2 %copy.41 = bf16[256,8,8,128]{3,2,1,0:T(8,128)(2,1)} copy(bf16[256,8,8,128]{3,1,2,0:T(8,128)(2,1)} %bitcast.127) | data formatting | bytes 8388608
  60.7 81.1 %all-gather.6.cloned.1.call-done = bf16[64,32768]{1,0:T(8,128)(2,1)} async-done(((bf16[64,512]{1,0:T(8,128)(2,1)}), bf16[64,32768]{1,0:T(8,128)(2,1)}) %all-gather.6.cloned.1.call-update) | async-done | bytes 4194320 | tf_op jit(solution)/shard_map/all_gather | solution.py:18
  141.8 7.8 %reshape.92 = bf16[64,64,4,128]{3,2,1,0:T(4,128)(2,1)} reshape(bf16[64,32768]{1,0:T(8,128)(2,1)} %all-gather.6.cloned.1.call-done) | data formatting | bytes 8388608 | tf_op jit(solution)/shard_map/reshape | solution.py:19
  149.6 9.0 %copy.29 = bf16[64,64,4,128]{3,0,2,1:T(8,128)(2,1)} copy(bf16[64,64,4,128]{3,2,1,0:T(4,128)(2,1)} %reshape.92) | data formatting | bytes 8388608 | tf_op jit(solution)/shard_map/reshape | solution.py:19
  158.6 3.0 gather_fusion.1
  161.8 1.0 gather_fusion.2
  162.7 7.6 %fusion.9 = f32[16,8,64,128]{3,2,1,0:T(8,128)} fusion(bf16[16,128,8,128]{3,2,1,0:T(8,128)(2,1)} %bitcast.128, bf16[16,8,64,128]{3,2,1,0:T(8,128)(2,1)S(1)} %bitcast.131, pred[16,8]{1,0:T(8,128)(4,1)S(1)} %copy.28, f32[16,128]{1,0:T(8,128)S(1)} %convert_bitcast_fusion, pred[16,128]{1,0:T(8,128)(4,1)S(1)} %compare_bitcast_fusion), kind=kOutput, calls=%fused_computation.15 | convolution fusion | flops 538705920 | bytes 10496128 | tf_op jit(solution)/shard_map/bpi,bikc->bkpc/dot_general | solution.py:46
  170.3 10.1 %scatter_custom_fusion = f32[64,8192]{1,0:T(8,128)S(1)} fusion(s32[128]{0:T(128)S(1)} %reshape.141, f32[16,8,64,128]{3,2,1,0:T(8,128)} %fusion.9, f32[]{:T(128)} %constant.42.clone.1), kind=kCustom, calls=%fused_computation.6 | custom fusion | flops 1048576 | bytes 6291460 | tf_op jit(solution)/shard_map/scatter-add | solution.py:50
  180.5 1.7 copy.43
  182.2 8.2 %all-to-all-start = ((f32[64,64,128]{2,1,0:T(8,128)}), f32[64,64,128]{2,1,0:T(8,128)S(1)}, u32[]{:S(2)}, u32[]{:S(2)}) async-start(f32[64,64,128]{2,1,0:T(8,128)} %bitcast.126), calls=%async_computation | async-start | bytes 4194304 | tf_op jit(solution)/shard_map/all_to_all | solution.py:52
  190.7 49.5 %all-to-all-done = f32[64,64,128]{2,1,0:T(8,128)S(1)} async-done(((f32[64,64,128]{2,1,0:T(8,128)}), f32[64,64,128]{2,1,0:T(8,128)S(1)}, u32[]{:S(2)}, u32[]{:S(2)}) %all-to-all-start) | async-done | bytes 2097184 | tf_op jit(solution)/shard_map/all_to_all | solution.py:52
  240.1 2.0 fusion.14
  242.1 0.8 fusion.101
  243.5 79.5 %all-gather.8.cloned.1.call-done = bf16[64,32768]{1,0:T(8,128)(2,1)} async-done(((bf16[64,512]{1,0:T(8,128)(2,1)}), bf16[64,32768]{1,0:T(8,128)(2,1)}) %all-gather.8.cloned.1.call-update) | async-done | bytes 4194320 | tf_op jit(solution)/shard_map/all_gather | solution.py:18
  323.0 7.8 %reshape.97 = bf16[64,64,4,128]{3,2,1,0:T(4,128)(2,1)} reshape(bf16[64,32768]{1,0:T(8,128)(2,1)} %all-gather.8.cloned.1.call-done) | data formatting | bytes 8388608 | tf_op jit(solution)/shard_map/reshape | solution.py:19
  330.7 9.0 %copy.35 = bf16[64,64,4,128]{3,0,2,1:T(8,128)(2,1)} copy(bf16[64,64,4,128]{3,2,1,0:T(4,128)(2,1)} %reshape.97) | data formatting | bytes 8388608 | tf_op jit(solution)/shard_map/reshape | solution.py:19
  339.7 3.0 gather_fusion.3
  342.9 1.0 gather_fusion.4
  343.8 3.9 fusion.82
  347.8 124.3 %all-reduce = (f32[64]{0:T(128)S(1)}, f32[]{:T(128)}) all-reduce(f32[64]{0:T(128)S(1)} %fusion.82, f32[]{:T(128)} %get-tuple-element.6), channel_id=1, replica_groups=mesh['dom'=8,'dp'=64] {'dp'}, use_global_device_ids=true, to_apply=%region_2.5 | all-reduce | flops 65 | bytes 520 | tf_op jit(solution)/shard_map/psum | solution.py:64
  (36 shorter events, 4.2 us)
Async XLA Ops:
  7.2 44.3 %all-gather.4.cloned.1.call-start = ((), (), s32[]{:S(2)}) async-start(), calls=%async_computation.1 | async-start | bytes 1179648 | tf_op jit(solution)/shard_map/all_gather | solution.py:32
  7.9 133.9 %all-gather.6.cloned.1.call-start = ((), (), s32[]{:S(2)}) async-start(), calls=%async_computation.2 | async-start | bytes 4259840 | tf_op jit(solution)/shard_map/all_gather | solution.py:18
  55.0 5.3 %copy-start = (s32[16,8]{0,1:T(8,128)S(1)}, s32[16,8]{0,1:T(8,128)}, u32[]{:S(2)}) copy-start(s32[16,8]{0,1:T(8,128)} %param.14) | copy-start | bytes 1540
  55.0 5.6 %copy-start.2 = (s32[64,64]{1,0:T(8,128)S(1)}, s32[64,64]{1,0:T(8,128)}, u32[]{:S(2)}) copy-start(s32[64,64]{1,0:T(8,128)} %param.13) | copy-start | bytes 49156
  55.0 5.6 %copy-start.1 = (s32[2048]{0:T(1024)S(1)}, s32[2048]{0:T(1024)}, u32[]{:S(2)}) copy-start(s32[2048]{0:T(1024)} %param.17) | copy-start | bytes 24580
  55.1 5.6 %copy-start.3 = (s32[2048]{0:T(1024)S(1)}, s32[2048]{0:T(1024)}, u32[]{:S(2)}) copy-start(s32[2048]{0:T(1024)} %param.16) | copy-start | bytes 24580
  182.2 58.0 %all-to-all-start = ((f32[64,64,128]{2,1,0:T(8,128)}), f32[64,64,128]{2,1,0:T(8,128)S(1)}, u32[]{:S(2)}, u32[]{:S(2)}) async-start(f32[64,64,128]{2,1,0:T(8,128)} %bitcast.126), calls=%async_computation | async-start | bytes 4194304 | tf_op jit(solution)/shard_map/all_to_all | solution.py:52
  190.4 132.5 %all-gather.8.cloned.1.call-start = ((), (), s32[]{:S(2)}) async-start(), calls=%async_computation.3 | async-start | bytes 4259840 | tf_op jit(solution)/shard_map/all_gather | solution.py:18
Sparse Core Ops, SparseCore 0:
  10.0 41.4 all-gather.3
  55.3 86.4 all-gather.5
  243.0 79.9 all-gather.7
where the time goes:
time: 484 us; the launch traced here: 480 us
  waiting for transfers between devices  253 us (52%)
  blocking collectives  124 us (26%)
  local copies, waits for them, and re-layouts  51.6 us (11%)
  between operations  14.6 us (3%)
  other arithmetic  14.5 us (3%)
  matrix products  13.5 us (3%)
  starting transfers between devices  8.35 us (2%)
    all_gather x2, waiting for transfers between devices, spread_blocks(): gathered = lax.all_gather(narrow, 'dp', axis=1, tiled=True)  161 us
    psum x1, blocking collectives, shards(): totals, counted = lax.psum((totals, counted), 'dp')  124 us
    all_to_all x1, waiting for transfers between devices, shards(): lax.all_to_all(outgoing, 'dp', split_axis=0, concat_axis=0, tiled=True)  49.5 us
    all_gather x1, waiting for transfers between devices, shards(): lineage = lax.all_gather(positions, 'dom', axis=0, tiled=True)  42.2 us
    reshape x4, local copies, waits for them, and re-layouts, spread_blocks(): gathered = gathered.reshape(particle_count, data_width, blocks_owned, TILE)  33.5 us
    scatter-add x1, other arithmetic, shards(): jax.ops.segment_sum(flat_terms, tile_slot.reshape(-1), num_segments=data_...  10.1 us
  transfers between devices with their start and end apart: 4, of which 4 were waited for; matrix products, arithmetic and copies ran while one was open for 2% of the time, Pallas kernels for 0%

commit v1 on v0

v1 whole, which is shorter than its diff:
```python
import functools

import jax
import jax.numpy as jnp
from jax import lax
from jax.experimental import pallas as pl
from jax.experimental.pallas import tpu as pltpu
from jax.sharding import Mesh, PartitionSpec as P

TILE = 128
CURRENT = 2
step_size = 1.0
prior_precision = 0.05

f32 = jnp.float32
bf16 = jnp.bfloat16
f16 = jnp.float16

VMEM = pltpu.VMEM
SMEM = pltpu.SMEM


def vspec():
    return pl.BlockSpec(memory_space=VMEM)


def sspec():
    return pl.BlockSpec(memory_space=SMEM)


def params(mib):
    return pltpu.CompilerParams(vmem_limit_bytes=mib << 20)


def exchange(x, axes):
    return lax.all_to_all(x, axes, split_axis=0, concat_axis=0, tiled=True)


def resample_kernel(anc, row, lineage, resampled, outgoing, blocks):
    particles, width = resampled.shape
    owned = width // TILE

    def pick(i, carry):
        resampled[pl.ds(i, 1), :] = lineage[pl.ds(anc[i], 1), :]
        return carry

    lax.fori_loop(0, particles, pick, 0, unroll=8)
    for q in range(owned):
        blocks[q] = resampled[:, q * TILE : (q + 1) * TILE].astype(bf16)

    def send(d, carry):
        outgoing[d] = blocks[row[d]]
        return carry

    lax.fori_loop(0, outgoing.shape[0], send, 0, unroll=8)


def weights_of(slot, fetched, b, per_block):
    return jnp.concatenate([fetched[slot[b, k]] for k in range(per_block)], axis=1)


def logits_of(weights, tiles):
    return lax.dot_general(
        weights, tiles, (((1,), (1,)), ((), ())), preferred_element_type=f32
    )


def design_copy(design, held, sems, b):
    rows = pl.ds(pl.multiple_of(b * TILE, TILE), TILE)
    return pltpu.make_async_copy(design.at[rows], held.at[rows], sems.at[b])


def gradient_kernel(slot, design, fetched, labels, sections, outgoing, total, held, sems):
    row_blocks, per_block = slot.shape
    for b in range(row_blocks):
        design_copy(design, held, sems, b).start()
    total[...] = jnp.zeros_like(total)

    def block(b, carry):
        design_copy(design, held, sems, b).wait()
        tiles = held[pl.ds(pl.multiple_of(b * TILE, TILE), TILE), :]
        logits = logits_of(weights_of(slot, fetched, b, per_block), tiles)
        target = labels[pl.ds(b, 1), :].astype(f32)
        active = sections[pl.ds(b, 1), :] <= CURRENT
        residual = jnp.where(active, target - jax.nn.sigmoid(logits), 0.0).astype(bf16)
        terms = jnp.dot(residual, tiles, preferred_element_type=f32)
        for k in range(per_block):
            j = slot[b, k]
            total[j] += terms[:, k * TILE : (k + 1) * TILE]
        return carry

    lax.fori_loop(0, row_blocks, block, 0)
    outgoing[...] = total[...]


def advance_kernel(row, column, resampled, incoming, advanced, outgoing, total, blocks):
    particles, width = resampled.shape
    owned = width // TILE
    total[...] = jnp.zeros_like(total)

    def add(s, carry):
        q = column[s]
        total[q] += incoming[s].astype(f32)
        return carry

    lax.fori_loop(0, incoming.shape[0], add, 0, unroll=4)
    for q in range(owned):
        lanes = slice(q * TILE, (q + 1) * TILE)
        old = resampled[:, lanes]
        new = old + step_size * (total[q] - prior_precision * old)
        advanced[:, lanes] = new
        blocks[q] = new.astype(bf16)

    def send(d, carry):
        outgoing[d] = blocks[row[d]]
        return carry

    lax.fori_loop(0, outgoing.shape[0], send, 0, unroll=8)


def likelihood_kernel(slot, design, fetched, labels, sections, outgoing, held, sems):
    row_blocks, per_block = slot.shape
    particles = fetched.shape[1]
    for b in range(row_blocks):
        design_copy(design, held, sems, b).start()

    def block(b, carry):
        total, counted = carry
        design_copy(design, held, sems, b).wait()
        tiles = held[pl.ds(pl.multiple_of(b * TILE, TILE), TILE), :]
        logits = logits_of(weights_of(slot, fetched, b, per_block), tiles)
        target = labels[pl.ds(b, 1), :].astype(f32)
        chosen = sections[pl.ds(b, 1), :] == CURRENT + 1
        soft = jnp.maximum(logits, 0.0) + jnp.log1p(jnp.exp(-jnp.abs(logits)))
        total += jnp.where(chosen, target * logits - soft, 0.0)
        counted += chosen.astype(f32)
        return total, counted

    total, counted = lax.fori_loop(
        0,
        row_blocks,
        block,
        (jnp.zeros((particles, TILE), f32), jnp.zeros((1, TILE), f32)),
    )
    rows = jnp.concatenate([total, jnp.broadcast_to(counted, (TILE - particles, TILE))], axis=0)
    sums = jnp.sum(rows.T, axis=0, keepdims=True)
    outgoing[...] = jnp.broadcast_to(sums[None], outgoing.shape)


def shards(data_axes, positions, ancestors, block_choice, tile_slot, design, labels, row_section):
    data_width = lax.axis_size(data_axes)
    device_index = lax.axis_index(data_axes)
    groups = lax.axis_size("dom")
    particles, width = positions.shape
    owned = width // TILE
    row_blocks, per_block = tile_slot.shape
    column = lax.dynamic_index_in_dim(block_choice, device_index, 1, keepdims=False)
    labels = labels.reshape(row_blocks, TILE)
    sections = row_section.reshape(row_blocks, TILE)

    spread = jnp.broadcast_to(positions[None], (groups, particles, width))
    lineage = exchange(spread, "dom").reshape(groups * particles, width)
    block_shape = (data_width, particles, TILE)
    resampled, outgoing = pl.pallas_call(
        resample_kernel,
        out_shape=(
            jax.ShapeDtypeStruct((particles, width), f32),
            jax.ShapeDtypeStruct(block_shape, bf16),
        ),
        in_specs=[sspec(), sspec(), vspec()],
        out_specs=(vspec(), vspec()),
        scratch_shapes=[VMEM((owned, particles, TILE), bf16)],
        compiler_params=params(8),
    )(ancestors, column, lineage)
    fetched = exchange(outgoing, data_axes)
    terms = pl.pallas_call(
        gradient_kernel,
        out_shape=jax.ShapeDtypeStruct(block_shape, f32),
        in_specs=[sspec(), pl.BlockSpec(memory_space=pl.ANY), vspec(), vspec(), vspec()],
        out_specs=vspec(),
        scratch_shapes=[
            VMEM(block_shape, f32),
            VMEM(design.shape, bf16),
            pltpu.SemaphoreType.DMA((row_blocks,)),
        ],
        compiler_params=params(16),
    )(tile_slot, design, fetched, labels, sections)
    incoming = exchange(terms.astype(f16), data_axes).astype(f32)
    advanced, outgoing = pl.pallas_call(
        advance_kernel,
        out_shape=(
            jax.ShapeDtypeStruct((particles, width), f32),
            jax.ShapeDtypeStruct(block_shape, bf16),
        ),
        in_specs=[sspec(), sspec(), vspec(), vspec()],
        out_specs=(vspec(), vspec()),
        scratch_shapes=[
            VMEM((owned, particles, TILE), f32),
            VMEM((owned, particles, TILE), bf16),
        ],
        compiler_params=params(8),
    )(column, column, resampled, incoming)
    fetched_new = exchange(outgoing, data_axes)
    sums = pl.pallas_call(
        likelihood_kernel,
        out_shape=jax.ShapeDtypeStruct((data_width, 1, TILE), f32),
        in_specs=[sspec(), pl.BlockSpec(memory_space=pl.ANY), vspec(), vspec(), vspec()],
        out_specs=vspec(),
        scratch_shapes=[
            VMEM(design.shape, bf16),
            pltpu.SemaphoreType.DMA((row_blocks,)),
        ],
        compiler_params=params(12),
    )(tile_slot, design, fetched_new, labels, sections)
    sums = jnp.sum(exchange(sums, data_axes), axis=(0, 1))
    return advanced, sums[:particles] / jnp.maximum(sums[particles], 1.0)


def solution(mesh):
    return jax.shard_map(
        functools.partial(shards, "dp"),
        mesh=mesh,
        in_specs=(P("dom", "dp"), P("dom"), P(), P("dp", None), P("dp", None), P("dp"), P("dp")),
        out_specs=(P("dom", "dp"), P("dom")),
        check_vma=False,
    )
```

time: 484 us -> 187 us (0.39)
  waiting for transfers between devices: 253 us -> 55.1 us
  local copies, waits for them, and re-layouts: 51.6 us -> 5.06 us
  blocking collectives: 124 us -> 84 us
  Pallas kernels: 0 us -> 16.8 us
  starting transfers between devices: 8.35 us -> 23.4 us
  matrix products: 13.5 us -> 0 us
  other arithmetic: 14.5 us -> 1.04 us
  between operations: 14.6 us -> 1.4 us
    all_gather x3 -> x0, waiting for transfers between devices: 203 us -> none  [the longest x2 161 us: spread_blocks(): gathered = lax.all_gather(narrow, 'dp', axis=1, tiled=True)]
    psum x1 -> x0, blocking collectives: 124 us -> none  [shards(): totals, counted = lax.psum((totals, counted), 'dp')]
    all_to_all x0 -> x3, blocking collectives: none -> 84 us  [exchange(): return lax.all_to_all(x, axes, split_axis=0, concat_axis=0, tiled=True)]
    reshape x4 -> x0, local copies, waits for them, and re-layouts: 33.5 us -> none  [spread_blocks(): gathered = gathered.reshape(particle_count, data_width, blocks_owned, TILE)]
    pallas_call x0 -> x4, Pallas kernels: none -> 16.8 us  [the longest x1 8.22 us: shards(): pl.pallas_call(gradient_kernel, out_shape=jax.ShapeDtypeStruct(block_shap...]
    all_to_all x1 -> x2, starting transfers between devices: 8.24 us -> 23.4 us  [exchange(): return lax.all_to_all(x, axes, split_axis=0, concat_axis=0, tiled=True)]
    dot_general x3 -> x0, matrix products: 13.5 us -> none  [the longest x1 7.63 us: shards(): jnp.einsum('bpi,bikc->bkpc', residual, design_tiles, preferred_element_ty...]
    scatter-add x1 -> x0, other arithmetic: 10.1 us -> none  [shards(): jax.ops.segment_sum(flat_terms, tile_slot.reshape(-1), num_segments=data_...]
  transfers between devices with their start and end apart: 4 -> 2, of which waited for: 4 -> 2; matrix products, arithmetic and copies ran while one was open for 2% -> 0% of each run, Pallas kernels for 0% -> 0%
where the time goes in v1:
time: 187 us
  blocking collectives  84 us (45%)
  waiting for transfers between devices  55.1 us (29%)
  starting transfers between devices  23.4 us (13%)
  Pallas kernels  16.8 us (9%)
  local copies, waits for them, and re-layouts  5.06 us (3%)
    all_to_all x3, blocking collectives, exchange(): return lax.all_to_all(x, axes, split_axis=0, concat_axis=0, tiled=True)  84 us
    all_to_all x2, waiting for transfers between devices, exchange(): return lax.all_to_all(x, axes, split_axis=0, concat_axis=0, tiled=True)  55.1 us
    all_to_all x2, starting transfers between devices, exchange(): return lax.all_to_all(x, axes, split_axis=0, concat_axis=0, tiled=True)  23.4 us
    pallas_call x1, Pallas kernels, shards(): pl.pallas_call(gradient_kernel, out_shape=jax.ShapeDtypeStruct(block_shap...  8.22 us
    pallas_call x1, Pallas kernels, shards(): pl.pallas_call(likelihood_kernel, out_shape=jax.ShapeDtypeStruct((data_wi...  4.99 us
  transfers between devices with their start and end apart: 2, of which 2 were waited for; matrix products, arithmetic and copies ran while one was open for 0% of the time, Pallas kernels for 0%

profile of v1, /device:TPU:1, one launch (start us, length us, event | category | flops | bytes accessed | tf_op | source)
XLA Modules:
  0.0 186.7 jit_solution(15296335037726798970)
XLA Ops:
  0.6 0.0 copy-start
  0.7 2.0 %broadcast_in_dim.2 = f32[8,64,512]{2,1,0:T(8,128)} broadcast(f32[64,512]{1,0:T(8,128)} %param.7), dimensions={1,2} | broadcast | bytes 1179648 | tf_op jit(solution)/shard_map/broadcast_in_dim | solution.py:161
  2.7 7.6 %all-to-all-start = ((f32[8,64,512]{2,1,0:T(8,128)}), f32[8,64,512]{2,1,0:T(8,128)S(1)}, u32[]{:S(2)}, u32[]{:S(2)}) async-start(f32[8,64,512]{2,1,0:T(8,128)} %broadcast_in_dim.2), calls=%async_computation | async-start | bytes 2097152 | tf_op jit(solution)/shard_map/all_to_all | solution.py:36
  10.3 0.0 copy-start.3
  10.3 0.0 copy-start.4
  10.3 0.2 dynamic-slice_reduce_fusion.row.column
  10.5 27.1 %all-to-all-done = f32[8,64,512]{2,1,0:T(8,128)S(1)} async-done(((f32[8,64,512]{2,1,0:T(8,128)}), f32[8,64,512]{2,1,0:T(8,128)S(1)}, u32[]{:S(2)}, u32[]{:S(2)}) %all-to-all-start) | async-done | bytes 1048608 | tf_op jit(solution)/shard_map/all_to_all | solution.py:36
  37.6 1.9 shard_map.86
  39.5 15.7 %all-to-all-start.1 = ((bf16[64,64,128]{2,1,0:T(8,128)(2,1)}), bf16[64,64,128]{2,1,0:T(8,128)(2,1)S(1)}, u32[]{:S(2)}, u32[]{:S(2)}) async-start(bf16[64,64,128]{2,1,0:T(8,128)(2,1)} %get-tuple-element.7), calls=%async_computation.1 | async-start | bytes 2097152 | tf_op jit(solution)/shard_map/all_to_all | solution.py:36
  55.2 0.1 copy.11.slot
  55.3 28.1 %all-to-all-done.1.fetched = bf16[64,64,128]{2,1,0:T(8,128)(2,1)S(1)} async-done(((bf16[64,64,128]{2,1,0:T(8,128)(2,1)}), bf16[64,64,128]{2,1,0:T(8,128)(2,1)S(1)}, u32[]{:S(2)}, u32[]{:S(2)}) %all-to-all-start.1) | async-done | bytes 1048608 | tf_op jit(solution)/shard_map/all_to_all | solution.py:36
  83.4 2.2 %copy-done.1 = bf16[2048,1024]{1,0:T(8,128)(2,1)S(1)} copy-done((bf16[2048,1024]{1,0:T(8,128)(2,1)S(1)}, bf16[2048,1024]{1,0:T(8,128)(2,1)}, u32[]{:S(2)}) %copy-start.1) | copy-done | bytes 4194328
  85.6 8.2 %shard_map.87 = f32[64,64,128]{2,1,0:T(8,128)S(1)} custom-call(s32[16,8]{1,0:T(8,128)S(1)} %copy.11.slot, bf16[2048,1024]{1,0:T(8,128)(2,1)S(1)} %copy-done.1, bf16[64,64,128]{2,1,0:T(8,128)(2,1)S(1)} %all-to-all-done.1.fetched, s32[16,128]{1,0:T(8,128)S(1)} %bitcast.5, s32[16,128]{1,0:T(8,128)S(1)} %bitcast.7), custom_call_target="tpu_custom_call" | custom-call | tf_op jit(solution)/shard_map/pallas_call | solution.py:176
  93.8 0.2 convert_element_type.6
  94.0 34.2 %all_to_all.25 = f16[64,64,128]{2,1,0:T(8,128)(2,1)S(1)} all-to-all(f16[64,64,128]{2,1,0:T(8,128)(2,1)S(1)} %convert_element_type.6), channel_id=1, replica_groups=mesh['dom'=8,'dp'=64] {'dp'}, dimensions={0} | all-to-all | bytes 2097152 | tf_op jit(solution)/shard_map/all_to_all | solution.py:36
  128.3 0.2 convert_element_type.7.incoming
  128.5 0.0 copy-start.2
  128.5 1.7 shard_map.88
  130.2 34.2 %all_to_all.26.fetched = bf16[64,64,128]{2,1,0:T(8,128)(2,1)S(1)} all-to-all(bf16[64,64,128]{2,1,0:T(8,128)(2,1)S(1)} %get-tuple-element.9), channel_id=1, replica_groups=mesh['dom'=8,'dp'=64] {'dp'}, dimensions={0} | all-to-all | bytes 2097152 | tf_op jit(solution)/shard_map/all_to_all | solution.py:36
  164.4 5.0 %shard_map.89 = f32[64,1,128]{2,1,0:T(1,128)S(1)} custom-call(s32[16,8]{1,0:T(8,128)S(1)} %copy.11.slot, bf16[2048,1024]{1,0:T(8,128)(2,1)S(1)} %copy-done.2, bf16[64,64,128]{2,1,0:T(8,128)(2,1)S(1)} %all_to_all.26.fetched, s32[16,128]{1,0:T(8,128)S(1)} %bitcast.6, s32[16,128]{1,0:T(8,128)S(1)} %bitcast.8), custom_call_target="tpu_custom_call" | custom-call | tf_op jit(solution)/shard_map/pallas_call | solution.py:204
  169.4 15.5 %all_to_all.27 = f32[64,1,128]{2,1,0:T(1,128)S(1)} all-to-all(f32[64,1,128]{2,1,0:T(1,128)S(1)} %shard_map.89), channel_id=1, replica_groups=mesh['dom'=8,'dp'=64] {'dp'}, dimensions={0} | all-to-all | bytes 65536 | tf_op jit(solution)/shard_map/all_to_all | solution.py:36
  184.9 0.1 reduce_sum.9
  185.0 0.6 slice.7
  186.2 0.5 slice_divide_fusion
  (9 shorter events, 0.0 us)
Async XLA Ops:
  0.6 9.7 %copy-start = (s32[64,64]{1,0:T(8,128)S(1)}, s32[64,64]{1,0:T(8,128)}, u32[]{:S(2)}) copy-start(s32[64,64]{1,0:T(8,128)} %param.9) | copy-start | bytes 49156
  0.6 36.9 %copy-start.5 = (s32[64]{0:T(128)S(1)}, s32[64]{0:T(128)}, u32[]{:S(2)}) copy-start(s32[64]{0:T(128)} %anc.1) | copy-start | bytes 772
  2.7 34.9 %all-to-all-start = ((f32[8,64,512]{2,1,0:T(8,128)}), f32[8,64,512]{2,1,0:T(8,128)S(1)}, u32[]{:S(2)}, u32[]{:S(2)}) async-start(f32[8,64,512]{2,1,0:T(8,128)} %broadcast_in_dim.2), calls=%async_computation | async-start | bytes 2097152 | tf_op jit(solution)/shard_map/all_to_all | solution.py:36
  10.3 44.9 %copy-start.6 = (s32[16,8]{0,1:T(8,128)S(1)}, s32[16,8]{0,1:T(8,128)}, u32[]{:S(2)}) copy-start(s32[16,8]{0,1:T(8,128)} %param.10) | copy-start | bytes 1540
  10.3 73.1 %copy-start.3 = (s32[2048]{0:T(1024)S(1)}, s32[2048]{0:T(1024)}, u32[]{:S(2)}) copy-start(s32[2048]{0:T(1024)} %param.12) | copy-start | bytes 24580
  10.3 73.0 %copy-start.4 = (s32[2048]{0:T(1024)S(1)}, s32[2048]{0:T(1024)}, u32[]{:S(2)}) copy-start(s32[2048]{0:T(1024)} %param.13) | copy-start | bytes 24580
  39.5 43.9 %all-to-all-start.1 = ((bf16[64,64,128]{2,1,0:T(8,128)(2,1)}), bf16[64,64,128]{2,1,0:T(8,128)(2,1)S(1)}, u32[]{:S(2)}, u32[]{:S(2)}) async-start(bf16[64,64,128]{2,1,0:T(8,128)(2,1)} %get-tuple-element.7), calls=%async_computation.1 | async-start | bytes 2097152 | tf_op jit(solution)/shard_map/all_to_all | solution.py:36
  83.4 2.2 %copy-start.1 = (bf16[2048,1024]{1,0:T(8,128)(2,1)S(1)}, bf16[2048,1024]{1,0:T(8,128)(2,1)}, u32[]{:S(2)}) copy-start(bf16[2048,1024]{1,0:T(8,128)(2,1)} %design.3) | copy-start | bytes 12582916
  128.5 35.9 %copy-start.2 = (bf16[2048,1024]{1,0:T(8,128)(2,1)S(1)}, bf16[2048,1024]{1,0:T(8,128)(2,1)}, u32[]{:S(2)}) copy-start(bf16[2048,1024]{1,0:T(8,128)(2,1)} %design.3) | copy-start | bytes 12582916

commit v2 on v1

v2 whole, which is shorter than its diff:
```python
import jax
import jax.numpy as jnp
from jax import lax
from jax.experimental import pallas as pl
from jax.experimental.pallas import tpu as pltpu
from jax.sharding import PartitionSpec as P


TILE = 128
CURRENT = 2
CHUNKS = 4
step_size = 1.0
prior_precision = 0.05

f32 = jnp.float32
bf16 = jnp.bfloat16
f16 = jnp.float16

VMEM = pltpu.VMEM
SMEM = pltpu.SMEM


def vspec():
    return pl.BlockSpec(memory_space=VMEM)


def sspec():
    return pl.BlockSpec(memory_space=SMEM)


def params(mib):
    return pltpu.CompilerParams(vmem_limit_bytes=mib << 20)


def exchange(x, axes):
    return lax.all_to_all(x, axes, split_axis=0, concat_axis=0, tiled=True)


def send_blocks(me, choice, blocks, outgoing):
    def send(d, carry):
        outgoing[d] = blocks[choice[d, me[0]]]
        return carry

    lax.fori_loop(0, outgoing.shape[0], send, 0, unroll=8)


def select_kernel(me, choice, positions, outgoing, blocks):
    for q in range(blocks.shape[0]):
        blocks[q] = positions[:, q * TILE : (q + 1) * TILE].astype(bf16)
    send_blocks(me, choice, blocks, outgoing)


def weights_of(slot, fetched, b, per_block):
    return jnp.concatenate([fetched[slot[b, k]] for k in range(per_block)], axis=1)


def logits_of(weights, tiles):
    return lax.dot_general(
        weights, tiles, (((1,), (1,)), ((), ())), preferred_element_type=f32
    )


def chunk_copies(design, held, sems):
    rows = design.shape[0] // CHUNKS
    return [
        pltpu.make_async_copy(
            design.at[pl.ds(c * rows, rows)], held.at[pl.ds(c * rows, rows)], sems.at[c]
        )
        for c in range(CHUNKS)
    ]


def gradient_kernel(slot, design, fetched, labels, sections, outgoing, held, sems):
    row_blocks, per_block = slot.shape
    copies = chunk_copies(design, held, sems)
    for copy in copies:
        copy.start()
    outgoing[...] = jnp.zeros_like(outgoing)

    for b in range(row_blocks):
        if b % (row_blocks // CHUNKS) == 0:
            copies[b // (row_blocks // CHUNKS)].wait()
        tiles = held[b * TILE : (b + 1) * TILE, :]
        logits = logits_of(weights_of(slot, fetched, b, per_block), tiles)
        target = labels[b : b + 1, :].astype(f32)
        active = sections[b : b + 1, :] <= CURRENT
        residual = jnp.where(active, target - jax.nn.sigmoid(logits), 0.0).astype(bf16)
        terms = jnp.dot(residual, tiles, preferred_element_type=f32)
        for k in range(per_block):
            j = slot[b, k]
            outgoing[j] += terms[:, k * TILE : (k + 1) * TILE]


def advance_kernel(me, choice, positions, incoming, advanced, outgoing, total, blocks):
    total[...] = jnp.zeros_like(total)

    def add(s, carry):
        total[choice[s, me[0]]] += incoming[s].astype(f32)
        return carry

    lax.fori_loop(0, incoming.shape[0], add, 0, unroll=4)
    for q in range(blocks.shape[0]):
        lanes = slice(q * TILE, (q + 1) * TILE)
        old = positions[:, lanes]
        new = old + step_size * (total[q] - prior_precision * old)
        advanced[:, lanes] = new
        blocks[q] = new.astype(bf16)
    send_blocks(me, choice, blocks, outgoing)


def pick_kernel(group, ancestors, *refs):
    moved, (resampled, table, sems) = refs[:-3], refs[-3:]
    particles = resampled.shape[0]
    groups = len(moved)
    copies = [
        pltpu.make_async_copy(moved[k], table.at[pl.ds(k * particles, particles)], sems.at[k])
        for k in range(groups)
    ]
    for copy in copies:
        copy.start()
    for copy in copies:
        copy.wait()

    def pick(i, carry):
        a = ancestors[i]
        ahead = lax.rem(group[0] - lax.div(a, particles) + groups, groups)
        row = ahead * particles + lax.rem(a, particles)
        resampled[pl.ds(i, 1), :] = table[pl.ds(row, 1), :]
        return carry

    lax.fori_loop(0, particles, pick, 0, unroll=8)


def likelihood_kernel(slot, design, fetched, labels, sections, outgoing, held, sems):
    row_blocks, per_block = slot.shape
    particles = fetched.shape[1]
    copies = chunk_copies(design, held, sems)
    for copy in copies:
        copy.start()
    total = jnp.zeros((particles, TILE), f32)
    counted = jnp.zeros((1, TILE), f32)
    for b in range(row_blocks):
        if b % (row_blocks // CHUNKS) == 0:
            copies[b // (row_blocks // CHUNKS)].wait()
        tiles = held[b * TILE : (b + 1) * TILE, :]
        logits = logits_of(weights_of(slot, fetched, b, per_block), tiles)
        target = labels[b : b + 1, :].astype(f32)
        chosen = sections[b : b + 1, :] == CURRENT + 1
        soft = jnp.maximum(logits, 0.0) + jnp.log1p(jnp.exp(-jnp.abs(logits)))
        total += jnp.where(chosen, target * logits - soft, 0.0)
        counted += chosen.astype(f32)
    rows = jnp.concatenate([total, jnp.broadcast_to(counted, (TILE - particles, TILE))], axis=0)
    sums = jnp.sum(rows.T, axis=0, keepdims=True)
    outgoing[...] = jnp.broadcast_to(sums[None], outgoing.shape)


def shards(positions, ancestors, block_choice, tile_slot, design, labels, row_section):
    data_width = lax.axis_size("dp")
    groups = lax.axis_size("dom")
    me = lax.axis_index("dp").astype(jnp.int32).reshape(1)
    group = lax.axis_index("dom").astype(jnp.int32).reshape(1)
    particles, width = positions.shape
    owned = width // TILE
    row_blocks, _ = tile_slot.shape
    labels = labels.reshape(row_blocks, TILE)
    sections = row_section.reshape(row_blocks, TILE)
    block_shape = (data_width, particles, TILE)
    design = pltpu.with_memory_space_constraint(design, pltpu.HBM)

    outgoing = pl.pallas_call(
        select_kernel,
        out_shape=jax.ShapeDtypeStruct(block_shape, bf16),
        in_specs=[sspec(), sspec(), vspec()],
        out_specs=vspec(),
        scratch_shapes=[VMEM((owned, particles, TILE), bf16)],
        compiler_params=params(4),
    )(me, block_choice, positions)
    fetched = exchange(outgoing, "dp")
    terms = pl.pallas_call(
        gradient_kernel,
        out_shape=jax.ShapeDtypeStruct(block_shape, f32),
        in_specs=[sspec(), pl.BlockSpec(memory_space=pltpu.HBM), vspec(), vspec(), vspec()],
        out_specs=vspec(),
        scratch_shapes=[VMEM(design.shape, bf16), pltpu.SemaphoreType.DMA((CHUNKS,))],
        compiler_params=params(12),
    )(tile_slot, design, fetched, labels, sections)
    incoming = exchange(terms.astype(f16), "dp").astype(f32)
    moved, outgoing = pl.pallas_call(
        advance_kernel,
        out_shape=(
            jax.ShapeDtypeStruct((particles, width), f32),
            jax.ShapeDtypeStruct(block_shape, bf16),
        ),
        in_specs=[sspec(), sspec(), vspec(), vspec()],
        out_specs=(vspec(), vspec()),
        scratch_shapes=[
            VMEM((owned, particles, TILE), f32),
            VMEM((owned, particles, TILE), bf16),
        ],
        compiler_params=params(6),
    )(me, block_choice, positions, incoming)
    fetched_new = exchange(outgoing, "dp")
    everyone = [moved]
    for ahead in range(1, groups):
        ring = [(g, (g + ahead) % groups) for g in range(groups)]
        everyone.append(lax.ppermute(moved, "dom", ring))
    sums = pl.pallas_call(
        likelihood_kernel,
        out_shape=jax.ShapeDtypeStruct((data_width, 1, TILE), f32),
        in_specs=[sspec(), pl.BlockSpec(memory_space=pltpu.HBM), vspec(), vspec(), vspec()],
        out_specs=vspec(),
        scratch_shapes=[VMEM(design.shape, bf16), pltpu.SemaphoreType.DMA((CHUNKS,))],
        compiler_params=params(12),
    )(tile_slot, design, fetched_new, labels, sections)
    sums = jnp.sum(exchange(sums, "dp"), axis=0)
    spread = jnp.broadcast_to(sums[None], (groups, 1, TILE))
    table = exchange(spread, "dom")[:, 0]
    advanced = pl.pallas_call(
        pick_kernel,
        out_shape=jax.ShapeDtypeStruct((particles, width), f32),
        in_specs=[sspec(), sspec()] + [vspec()] * groups,
        out_specs=vspec(),
        scratch_shapes=[VMEM((groups * particles, width), f32), pltpu.SemaphoreType.DMA((groups,))],
        compiler_params=params(4),
    )(group, ancestors, *everyone)
    from_group = jnp.arange(groups)[None, :, None] == (ancestors // particles)[:, None, None]
    from_row = jnp.arange(TILE)[None, None, :] == (ancestors % particles)[:, None, None]
    totals = jnp.sum(jnp.where(from_group & from_row, table[None], 0.0), axis=(1, 2))
    return advanced, totals / jnp.maximum(sums[0, particles], 1.0)


def solution(mesh):
    return jax.shard_map(
        shards,
        mesh=mesh,
        in_specs=(P("dom", "dp"), P("dom"), P(), P("dp", None), P("dp", None), P("dp"), P("dp")),
        out_specs=(P("dom", "dp"), P("dom")),
        check_vma=False,
    )
```

time: 187 us -> 180 us (0.963)
  blocking collectives: 84 us -> 34.2 us
  starting transfers between devices: 23.4 us -> 62.3 us
  Pallas kernels: 16.8 us -> 20.4 us
    all_to_all x3 -> x1, blocking collectives: 84 us -> 34.2 us  [exchange(): return lax.all_to_all(x, axes, split_axis=0, concat_axis=0, tiled=True)]
    ppermute x0 -> x7, starting transfers between devices: none -> 31.6 us  [shards(): everyone.append(lax.ppermute(moved, 'dom', ring))]
    all_to_all x2 -> x4, starting transfers between devices: 23.4 us -> 30.7 us  [exchange(): return lax.all_to_all(x, axes, split_axis=0, concat_axis=0, tiled=True)]
    all_to_all x2 -> x4, waiting for transfers between devices: 55.1 us -> 48.8 us  [exchange(): return lax.all_to_all(x, axes, split_axis=0, concat_axis=0, tiled=True)]
    ppermute x0 -> x7, waiting for transfers between devices: none -> 5.89 us  [shards(): everyone.append(lax.ppermute(moved, 'dom', ring))]
    pallas_call x1 -> x2, Pallas kernels: 1.87 us -> 5.41 us  [the longest x1 3.18 us: shards(): pl.pallas_call(pick_kernel, out_shape=jax.ShapeDtypeStruct((particles, wi...]
  transfers between devices with their start and end apart: 2 -> 11, of which waited for: 2 -> 4; matrix products, arithmetic and copies ran while one was open for 0% -> 1% of each run, Pallas kernels for 0% -> 4%
where the time goes in v2:
time: 180 us; the launch traced here: 179 us
  starting transfers between devices  62.3 us (35%)
  waiting for transfers between devices  54.7 us (30%)
  blocking collectives  34.2 us (19%)
  Pallas kernels  20.4 us (11%)
  local copies, waits for them, and re-layouts  3.63 us (2%)
  other arithmetic  2.16 us (1%)
    all_to_all x4, waiting for transfers between devices, exchange(): return lax.all_to_all(x, axes, split_axis=0, concat_axis=0, tiled=True)  48.8 us
    all_to_all x1, blocking collectives, exchange(): return lax.all_to_all(x, axes, split_axis=0, concat_axis=0, tiled=True)  34.2 us
    ppermute x7, starting transfers between devices, shards(): everyone.append(lax.ppermute(moved, 'dom', ring))  31.6 us
    all_to_all x4, starting transfers between devices, exchange(): return lax.all_to_all(x, axes, split_axis=0, concat_axis=0, tiled=True)  30.7 us
    pallas_call x1, Pallas kernels, shards(): pl.pallas_call(gradient_kernel, out_shape=jax.ShapeDtypeStruct(block_shap...  7.63 us
    ppermute x7, waiting for transfers between devices, shards(): everyone.append(lax.ppermute(moved, 'dom', ring))  5.89 us
    pallas_call x1, Pallas kernels, shards(): pl.pallas_call(likelihood_kernel, out_shape=jax.ShapeDtypeStruct((data_wi...  4.71 us
  transfers between devices with their start and end apart: 11, of which 4 were waited for; matrix products, arithmetic and copies ran while one was open for 1% of the time, Pallas kernels for 4%

profile of v2, /device:TPU:1, one launch (start us, length us, event | category | flops | bytes accessed | tf_op | source)
XLA Modules:
  0.0 178.9 jit_solution(10087491713863171060)
XLA Ops:
  0.7 0.9 copy-done
  1.6 0.8 copy-done.2
  2.3 2.2 %shard_map.86 = bf16[64,64,128]{2,1,0:T(8,128)(2,1)} custom-call(s32[1]{0:T(128)} %bitcast.1.me, s32[64,64]{1,0:T(8,128)S(1)} %copy-done.2, f32[64,512]{1,0:T(8,128)S(1)} %copy-done), custom_call_target="tpu_custom_call" | custom-call | tf_op jit(solution)/shard_map/pallas_call | solution.py:170
  4.5 14.8 %all-to-all-start = ((bf16[64,64,128]{2,1,0:T(8,128)(2,1)}), bf16[64,64,128]{2,1,0:T(8,128)(2,1)S(1)}, u32[]{:S(2)}, u32[]{:S(2)}) async-start(bf16[64,64,128]{2,1,0:T(8,128)(2,1)} %shard_map.86), calls=%async_computation | async-start | bytes 2097152 | tf_op jit(solution)/shard_map/all_to_all | solution.py:36
  19.5 28.1 %all-to-all-done.fetched = bf16[64,64,128]{2,1,0:T(8,128)(2,1)S(1)} async-done(((bf16[64,64,128]{2,1,0:T(8,128)(2,1)}), bf16[64,64,128]{2,1,0:T(8,128)(2,1)S(1)}, u32[]{:S(2)}, u32[]{:S(2)}) %all-to-all-start) | async-done | bytes 1048608 | tf_op jit(solution)/shard_map/all_to_all | solution.py:36
  47.5 7.6 %shard_map.87 = f32[64,64,128]{2,1,0:T(8,128)S(1)} custom-call(s32[16,8]{1,0:T(8,128)S(1)} %copy.13.slot, bf16[2048,1024]{1,0:T(8,128)(2,1)} %design.3, bf16[64,64,128]{2,1,0:T(8,128)(2,1)S(1)} %all-to-all-done.fetched, s32[16,128]{1,0:T(8,128)S(1)} %bitcast.7, s32[16,128]{1,0:T(8,128)S(1)} %bitcast.9), custom_call_target="tpu_custom_call" | custom-call | tf_op jit(solution)/shard_map/pallas_call | solution.py:179
  55.4 34.2 %all_to_all.25 = f16[64,64,128]{2,1,0:T(8,128)(2,1)S(1)} all-to-all(f16[64,64,128]{2,1,0:T(8,128)(2,1)S(1)} %convert_element_type.6), channel_id=1, replica_groups=mesh['dom'=8,'dp'=64] {'dp'}, dimensions={0} | all-to-all | bytes 2097152 | tf_op jit(solution)/shard_map/all_to_all | solution.py:36
  90.6 2.6 %shard_map.88 = (f32[64,512]{1,0:T(8,128)S(1)}, bf16[64,64,128]{2,1,0:T(8,128)(2,1)}) custom-call(s32[1]{0:T(128)} %bitcast.1.me, s32[64,64]{1,0:T(8,128)S(1)} %copy-done.3, f32[64,512]{1,0:T(8,128)S(1)} %copy-done.1, f32[64,64,128]{2,1,0:T(8,128)S(1)} %convert_element_type.7.incoming), custom_call_target="tpu_custom_call" | custom-call | tf_op jit(solution)/shard_map/pallas_call | solution.py:188
  93.2 6.3 %all-to-all-start.2 = ((bf16[64,64,128]{2,1,0:T(8,128)(2,1)}), bf16[64,64,128]{2,1,0:T(8,128)(2,1)S(1)}, u32[]{:S(2)}, u32[]{:S(2)}) async-start(bf16[64,64,128]{2,1,0:T(8,128)(2,1)} %get-tuple-element.5), calls=%async_computation.2 | async-start | bytes 2097152 | tf_op jit(solution)/shard_map/all_to_all | solution.py:36
  99.5 3.2 %collective-permute-start = (f32[64,512]{1,0:T(8,128)S(1)}, f32[64,512]{1,0:T(8,128)S(1)}, u32[]{:S(2)}, u32[]{:S(2)}) collective-permute-start(f32[64,512]{1,0:T(8,128)S(1)} %get-tuple-element.4.refs_0_), channel_id=1, source_target_pairs={{0,64},{64,128},{128,192},{192,256},{256,320},{320,384},{384,448},... | collective-permute-start | bytes 393224 | tf_op jit(solution)/shard_map/ppermute | solution.py:206
  102.7 4.2 %collective-permute-start.1 = (f32[64,512]{1,0:T(8,128)S(1)}, f32[64,512]{1,0:T(8,128)S(1)}, u32[]{:S(2)}, u32[]{:S(2)}) collective-permute-start(f32[64,512]{1,0:T(8,128)S(1)} %get-tuple-element.4.refs_0_), channel_id=1, source_target_pairs={{0,128},{64,192},{128,256},{192,320},{256,384},{320,448},{384,0},{... | collective-permute-start | bytes 393224 | tf_op jit(solution)/shard_map/ppermute | solution.py:206
  107.0 20.7 %all-to-all-done.2.fetched = bf16[64,64,128]{2,1,0:T(8,128)(2,1)S(1)} async-done(((bf16[64,64,128]{2,1,0:T(8,128)(2,1)}), bf16[64,64,128]{2,1,0:T(8,128)(2,1)S(1)}, u32[]{:S(2)}, u32[]{:S(2)}) %all-to-all-start.2) | async-done | bytes 1048608 | tf_op jit(solution)/shard_map/all_to_all | solution.py:36
  127.7 4.7 %shard_map.90 = f32[64,1,128]{2,1,0:T(1,128)} custom-call(s32[16,8]{1,0:T(8,128)S(1)} %copy.13.slot, bf16[2048,1024]{1,0:T(8,128)(2,1)} %design.3, bf16[64,64,128]{2,1,0:T(8,128)(2,1)S(1)} %all-to-all-done.2.fetched, s32[16,128]{1,0:T(8,128)S(1)} %bitcast.8, s32[16,128]{1,0:T(8,128)S(1)} %bitcast.10), custom_call_target="tpu_custom_call" | custom-call | tf_op jit(solution)/shard_map/pallas_call | solution.py:207
  132.4 6.3 %all-to-all-start.3 = ((f32[64,1,128]{2,1,0:T(1,128)}), f32[64,1,128]{2,1,0:T(1,128)S(1)}, u32[]{:S(2)}, u32[]{:S(2)}) async-start(f32[64,1,128]{2,1,0:T(1,128)} %shard_map.90), calls=%async_computation.3 | async-start | bytes 65536 | tf_op jit(solution)/shard_map/all_to_all | solution.py:36
  138.7 5.2 %collective-permute-start.2 = (f32[64,512]{1,0:T(8,128)S(1)}, f32[64,512]{1,0:T(8,128)S(1)}, u32[]{:S(2)}, u32[]{:S(2)}) collective-permute-start(f32[64,512]{1,0:T(8,128)S(1)} %get-tuple-element.4.refs_0_), channel_id=1, source_target_pairs={{0,192},{64,256},{128,320},{192,384},{256,448},{320,0},{384,64},{4... | collective-permute-start | bytes 393224 | tf_op jit(solution)/shard_map/ppermute | solution.py:206
  144.0 4.8 %collective-permute-start.3 = (f32[64,512]{1,0:T(8,128)S(1)}, f32[64,512]{1,0:T(8,128)S(1)}, u32[]{:S(2)}, u32[]{:S(2)}) collective-permute-start(f32[64,512]{1,0:T(8,128)S(1)} %get-tuple-element.4.refs_0_), channel_id=1, source_target_pairs={{0,256},{64,320},{128,384},{192,448},{256,0},{320,64},{384,128},{4... | collective-permute-start | bytes 393224 | tf_op jit(solution)/shard_map/ppermute | solution.py:206
  148.8 5.8 %collective-permute-start.4 = (f32[64,512]{1,0:T(8,128)S(1)}, f32[64,512]{1,0:T(8,128)S(1)}, u32[]{:S(2)}, u32[]{:S(2)}) collective-permute-start(f32[64,512]{1,0:T(8,128)S(1)} %get-tuple-element.4.refs_0_), channel_id=1, source_target_pairs={{0,320},{64,384},{128,448},{192,0},{256,64},{320,128},{384,192},{4... | collective-permute-start | bytes 393224 | tf_op jit(solution)/shard_map/ppermute | solution.py:206
  155.2 3.3 %all-to-all-start.4 = ((f32[8,1,128]{2,1,0:T(1,128)}), f32[8,1,128]{2,1,0:T(1,128)S(1)}, u32[]{:S(2)}, u32[]{:S(2)}) async-start(f32[8,1,128]{2,1,0:T(1,128)} %broadcast_in_dim.24), calls=%async_computation.4 | async-start | bytes 8192 | tf_op jit(solution)/shard_map/all_to_all | solution.py:36
  158.6 5.4 %collective-permute-start.5 = (f32[64,512]{1,0:T(8,128)S(1)}, f32[64,512]{1,0:T(8,128)S(1)}, u32[]{:S(2)}, u32[]{:S(2)}) collective-permute-start(f32[64,512]{1,0:T(8,128)S(1)} %get-tuple-element.4.refs_0_), channel_id=1, source_target_pairs={{0,384},{64,448},{128,0},{192,64},{256,128},{320,192},{384,256},{4... | collective-permute-start | bytes 393224 | tf_op jit(solution)/shard_map/ppermute | solution.py:206
  164.0 3.1 %collective-permute-start.6 = (f32[64,512]{1,0:T(8,128)S(1)}, f32[64,512]{1,0:T(8,128)S(1)}, u32[]{:S(2)}, u32[]{:S(2)}) collective-permute-start(f32[64,512]{1,0:T(8,128)S(1)} %get-tuple-element.4.refs_0_), channel_id=1, source_target_pairs={{0,448},{64,0},{128,64},{192,128},{256,192},{320,256},{384,320},{4... | collective-permute-start | bytes 393224 | tf_op jit(solution)/shard_map/ppermute | solution.py:206
  167.2 3.8 %collective-permute-done.5.refs_6_ = f32[64,512]{1,0:T(8,128)S(1)} collective-permute-done((f32[64,512]{1,0:T(8,128)S(1)}, f32[64,512]{1,0:T(8,128)S(1)}, u32[]{:S(2)}, u32[]{:S(2)}) %collective-permute-start.5) | collective-permute-done | bytes 131104 | tf_op jit(solution)/shard_map/ppermute | solution.py:206
  171.0 2.0 %collective-permute-done.6.refs_7_ = f32[64,512]{1,0:T(8,128)S(1)} collective-permute-done((f32[64,512]{1,0:T(8,128)S(1)}, f32[64,512]{1,0:T(8,128)S(1)}, u32[]{:S(2)}, u32[]{:S(2)}) %collective-permute-start.6) | collective-permute-done | bytes 131104 | tf_op jit(solution)/shard_map/ppermute | solution.py:206
  173.0 3.2 %shard_map.89 = f32[64,512]{1,0:T(8,128)} custom-call(s32[1]{0:T(128)} %bitcast.group, s32[64]{0:T(128)S(1)} %copy-done.6, f32[64,512]{1,0:T(8,128)S(1)} %get-tuple-element.4.refs_0_, f32[64,512]{1,0:T(8,128)S(1)} %collective-permute-done.refs_1_, f32[64,512]{1,0:T(8,128)S(1)} %collective-permute-done.1.refs_2_, ...), custom_call_target="tpu_custom_call" | custom-call | tf_op jit(solution)/shard_map/pallas_call | solution.py:218
  177.5 0.9 select_reduce_fusion
  (31 shorter events, 3.2 us)
Async XLA Ops:
  0.6 18.7 %copy-start.7 = (s32[16,8]{0,1:T(8,128)S(1)}, s32[16,8]{0,1:T(8,128)}, u32[]{:S(2)}) copy-start(s32[16,8]{0,1:T(8,128)} %param.10) | copy-start | bytes 1540
  0.6 0.9 copy-start
  1.6 0.8 copy-start.2
  2.3 45.2 %copy-start.4 = (s32[2048]{0:T(1024)S(1)}, s32[2048]{0:T(1024)}, u32[]{:S(2)}) copy-start(s32[2048]{0:T(1024)} %param.12) | copy-start | bytes 24580
  2.3 45.2 %copy-start.5 = (s32[2048]{0:T(1024)S(1)}, s32[2048]{0:T(1024)}, u32[]{:S(2)}) copy-start(s32[2048]{0:T(1024)} %param.13) | copy-start | bytes 24580
  4.5 43.0 %all-to-all-start = ((bf16[64,64,128]{2,1,0:T(8,128)(2,1)}), bf16[64,64,128]{2,1,0:T(8,128)(2,1)S(1)}, u32[]{:S(2)}, u32[]{:S(2)}) async-start(bf16[64,64,128]{2,1,0:T(8,128)(2,1)} %shard_map.86), calls=%async_computation | async-start | bytes 2097152 | tf_op jit(solution)/shard_map/all_to_all | solution.py:36
  89.7 0.9 copy-start.1
  89.7 0.9 copy-start.3
  90.6 8.9 %copy-start.6 = (s32[64]{0:T(128)S(1)}, s32[64]{0:T(128)}, u32[]{:S(2)}) copy-start(s32[64]{0:T(128)} %ancestors.1) | copy-start | bytes 772
  93.2 34.4 %all-to-all-start.2 = ((bf16[64,64,128]{2,1,0:T(8,128)(2,1)}), bf16[64,64,128]{2,1,0:T(8,128)(2,1)S(1)}, u32[]{:S(2)}, u32[]{:S(2)}) async-start(bf16[64,64,128]{2,1,0:T(8,128)(2,1)} %get-tuple-element.5), calls=%async_computation.2 | async-start | bytes 2097152 | tf_op jit(solution)/shard_map/all_to_all | solution.py:36
  99.5 59.0 %collective-permute-start = (f32[64,512]{1,0:T(8,128)S(1)}, f32[64,512]{1,0:T(8,128)S(1)}, u32[]{:S(2)}, u32[]{:S(2)}) collective-permute-start(f32[64,512]{1,0:T(8,128)S(1)} %get-tuple-element.4.refs_0_), channel_id=1, source_target_pairs={{0,64},{64,128},{128,192},{192,256},{256,320},{320,384},{384,448},... | collective-permute-start | bytes 393224 | tf_op jit(solution)/shard_map/ppermute | solution.py:206
  102.7 61.2 %collective-permute-start.1 = (f32[64,512]{1,0:T(8,128)S(1)}, f32[64,512]{1,0:T(8,128)S(1)}, u32[]{:S(2)}, u32[]{:S(2)}) collective-permute-start(f32[64,512]{1,0:T(8,128)S(1)} %get-tuple-element.4.refs_0_), channel_id=1, source_target_pairs={{0,128},{64,192},{128,256},{192,320},{256,384},{320,448},{384,0},{... | collective-permute-start | bytes 393224 | tf_op jit(solution)/shard_map/ppermute | solution.py:206
  132.4 22.1 %all-to-all-start.3 = ((f32[64,1,128]{2,1,0:T(1,128)}), f32[64,1,128]{2,1,0:T(1,128)S(1)}, u32[]{:S(2)}, u32[]{:S(2)}) async-start(f32[64,1,128]{2,1,0:T(1,128)} %shard_map.90), calls=%async_computation.3 | async-start | bytes 65536 | tf_op jit(solution)/shard_map/all_to_all | solution.py:36
  138.7 28.4 %collective-permute-start.2 = (f32[64,512]{1,0:T(8,128)S(1)}, f32[64,512]{1,0:T(8,128)S(1)}, u32[]{:S(2)}, u32[]{:S(2)}) collective-permute-start(f32[64,512]{1,0:T(8,128)S(1)} %get-tuple-element.4.refs_0_), channel_id=1, source_target_pairs={{0,192},{64,256},{128,320},{192,384},{256,448},{320,0},{384,64},{4... | collective-permute-start | bytes 393224 | tf_op jit(solution)/shard_map/ppermute | solution.py:206
  144.0 23.2 %collective-permute-start.3 = (f32[64,512]{1,0:T(8,128)S(1)}, f32[64,512]{1,0:T(8,128)S(1)}, u32[]{:S(2)}, u32[]{:S(2)}) collective-permute-start(f32[64,512]{1,0:T(8,128)S(1)} %get-tuple-element.4.refs_0_), channel_id=1, source_target_pairs={{0,256},{64,320},{128,384},{192,448},{256,0},{320,64},{384,128},{4... | collective-permute-start | bytes 393224 | tf_op jit(solution)/shard_map/ppermute | solution.py:206
  148.8 18.4 %collective-permute-start.4 = (f32[64,512]{1,0:T(8,128)S(1)}, f32[64,512]{1,0:T(8,128)S(1)}, u32[]{:S(2)}, u32[]{:S(2)}) collective-permute-start(f32[64,512]{1,0:T(8,128)S(1)} %get-tuple-element.4.refs_0_), channel_id=1, source_target_pairs={{0,320},{64,384},{128,448},{192,0},{256,64},{320,128},{384,192},{4... | collective-permute-start | bytes 393224 | tf_op jit(solution)/shard_map/ppermute | solution.py:206
  155.2 22.3 %all-to-all-start.4 = ((f32[8,1,128]{2,1,0:T(1,128)}), f32[8,1,128]{2,1,0:T(1,128)S(1)}, u32[]{:S(2)}, u32[]{:S(2)}) async-start(f32[8,1,128]{2,1,0:T(1,128)} %broadcast_in_dim.24), calls=%async_computation.4 | async-start | bytes 8192 | tf_op jit(solution)/shard_map/all_to_all | solution.py:36
  158.6 12.5 %collective-permute-start.5 = (f32[64,512]{1,0:T(8,128)S(1)}, f32[64,512]{1,0:T(8,128)S(1)}, u32[]{:S(2)}, u32[]{:S(2)}) collective-permute-start(f32[64,512]{1,0:T(8,128)S(1)} %get-tuple-element.4.refs_0_), channel_id=1, source_target_pairs={{0,384},{64,448},{128,0},{192,64},{256,128},{320,192},{384,256},{4... | collective-permute-start | bytes 393224 | tf_op jit(solution)/shard_map/ppermute | solution.py:206
  164.0 9.1 %collective-permute-start.6 = (f32[64,512]{1,0:T(8,128)S(1)}, f32[64,512]{1,0:T(8,128)S(1)}, u32[]{:S(2)}, u32[]{:S(2)}) collective-permute-start(f32[64,512]{1,0:T(8,128)S(1)} %get-tuple-element.4.refs_0_), channel_id=1, source_target_pairs={{0,448},{64,0},{128,64},{192,128},{256,192},{320,256},{384,320},{4... | collective-permute-start | bytes 393224 | tf_op jit(solution)/shard_map/ppermute | solution.py:206

commit v3 on v2

v3 whole, which is shorter than its diff:
```python
import functools

import jax
import jax.numpy as jnp
from jax import lax
from jax.experimental import pallas as pl
from jax.experimental.pallas import tpu as pltpu
from jax.sharding import PartitionSpec as P


TILE = 128
CURRENT = 2
CHUNKS = 4
step_size = 1.0
prior_precision = 0.05

f32 = jnp.float32
bf16 = jnp.bfloat16
f16 = jnp.float16

VMEM = pltpu.VMEM
SMEM = pltpu.SMEM


def vspec():
    return pl.BlockSpec(memory_space=VMEM)


def sspec():
    return pl.BlockSpec(memory_space=SMEM)


def hspec():
    return pl.BlockSpec(memory_space=pltpu.HBM)


def params(mib):
    return pltpu.CompilerParams(vmem_limit_bytes=mib << 20)


def exchange(x, axes):
    return lax.all_to_all(x, axes, split_axis=0, concat_axis=0, tiled=True)


def select_kernel(me, choice, positions, outgoing, column, choice_here, here, blocks, sems):
    first = pltpu.make_async_copy(choice, choice_here, sems.at[0])
    second = pltpu.make_async_copy(positions, here, sems.at[1])
    first.start()
    second.start()
    second.wait()
    for q in range(blocks.shape[0]):
        blocks[q] = here[:, q * TILE : (q + 1) * TILE].astype(bf16)
    first.wait()

    def send(d, carry):
        chosen = choice_here[d, me[0]]
        column[d] = chosen
        outgoing[d] = blocks[chosen]
        return carry

    lax.fori_loop(0, outgoing.shape[0], send, 0, unroll=8)


def weights_of(slot, fetched, b, per_block):
    return jnp.concatenate([fetched[slot[k, b]] for k in range(per_block)], axis=1)


def logits_of(weights, tiles):
    return lax.dot_general(
        weights, tiles, (((1,), (1,)), ((), ())), preferred_element_type=f32
    )


def chunk_copies(design, held, sems):
    chunks = sems.shape[0]
    rows = design.shape[0] // chunks
    return [
        pltpu.make_async_copy(
            design.at[pl.ds(c * rows, rows)], held.at[pl.ds(c * rows, rows)], sems.at[c]
        )
        for c in range(chunks)
    ]


def gradient_kernel(slot, design, fetched, labels, sections, outgoing, held, sems):
    per_block, row_blocks = slot.shape
    copies = chunk_copies(design, held, sems)
    for copy in copies:
        copy.start()
    outgoing[...] = jnp.zeros_like(outgoing)

    def tiles_of(b):
        return held[b * TILE : (b + 1) * TILE, :]

    residuals = []
    for b in range(row_blocks):
        if b % (row_blocks // len(copies)) == 0:
            copies[b // (row_blocks // len(copies))].wait()
        logits = logits_of(weights_of(slot, fetched, b, per_block), tiles_of(b))
        target = labels[b : b + 1, :].astype(f32)
        active = sections[b : b + 1, :] <= CURRENT
        residual = jnp.where(active, target - jax.nn.sigmoid(logits), 0.0)
        residuals.append(residual.astype(bf16))
    for b in range(row_blocks):
        terms = jnp.dot(residuals[b], tiles_of(b), preferred_element_type=f32)
        for k in range(per_block):
            j = slot[k, b]
            outgoing[j] += terms[:, k * TILE : (k + 1) * TILE]


def advance_kernel(column, positions, incoming, advanced, outgoing, here, total, blocks, sem):
    copy = pltpu.make_async_copy(positions, here, sem)
    copy.start()
    total[...] = jnp.zeros_like(total)

    def add(s, carry):
        total[column[s]] += incoming[s].astype(f32)
        return carry

    lax.fori_loop(0, incoming.shape[0], add, 0, unroll=4)
    copy.wait()
    for q in range(blocks.shape[0]):
        lanes = slice(q * TILE, (q + 1) * TILE)
        old = here[:, lanes]
        new = old + step_size * (total[q] - prior_precision * old)
        advanced[:, lanes] = new
        blocks[q] = new.astype(bf16)

    def send(d, carry):
        outgoing[d] = blocks[column[d]]
        return carry

    lax.fori_loop(0, outgoing.shape[0], send, 0, unroll=8)


def pick_kernel(group, ancestors, *refs):
    moved, (resampled, table, sems) = refs[:-3], refs[-3:]
    particles = resampled.shape[0]
    groups = len(moved)
    copies = [
        pltpu.make_async_copy(moved[k], table.at[pl.ds(k * particles, particles)], sems.at[k])
        for k in range(groups)
    ]
    for copy in copies:
        copy.start()
    for copy in copies:
        copy.wait()

    def pick(i, carry):
        a = ancestors[i]
        ahead = lax.rem(group[0] - lax.div(a, particles) + groups, groups)
        row = ahead * particles + lax.rem(a, particles)
        resampled[pl.ds(i, 1), :] = table[pl.ds(row, 1), :]
        return carry

    lax.fori_loop(0, particles, pick, 0, unroll=8)


def likelihood_kernel(slot, design, fetched, labels, sections, outgoing, held, sems):
    per_block, row_blocks = slot.shape
    particles = fetched.shape[1]
    copies = chunk_copies(design, held, sems)
    for copy in copies:
        copy.start()
    total = jnp.zeros((particles, TILE), f32)
    counted = jnp.zeros((1, TILE), f32)
    for b in range(row_blocks):
        if b % (row_blocks // len(copies)) == 0:
            copies[b // (row_blocks // len(copies))].wait()
        tiles = held[b * TILE : (b + 1) * TILE, :]
        logits = logits_of(weights_of(slot, fetched, b, per_block), tiles)
        target = labels[b : b + 1, :].astype(f32)
        chosen = sections[b : b + 1, :] == CURRENT + 1
        soft = jnp.maximum(logits, 0.0) + jnp.log1p(jnp.exp(-jnp.abs(logits)))
        total += jnp.where(chosen, target * logits - soft, 0.0)
        counted += chosen.astype(f32)
    rows = jnp.concatenate([total, jnp.broadcast_to(counted, (TILE - particles, TILE))], axis=0)
    sums = jnp.sum(rows.T, axis=0, keepdims=True)
    outgoing[...] = jnp.broadcast_to(sums[None], outgoing.shape)


def mean_kernel(particles, sums, means):
    total = jnp.sum(sums[...], axis=0)
    count = jnp.maximum(total[:, particles : particles + 1], 1.0)
    means[...] = jnp.broadcast_to((total / count)[None], means.shape)


def shards(positions, ancestors, block_choice, tile_slot, design, labels, row_section):
    data_width = lax.axis_size("dp")
    groups = lax.axis_size("dom")
    me = lax.axis_index("dp").astype(jnp.int32).reshape(1)
    group = lax.axis_index("dom").astype(jnp.int32).reshape(1)
    particles, width = positions.shape
    owned = width // TILE
    row_blocks = tile_slot.shape[0]
    labels = labels.reshape(row_blocks, TILE)
    sections = row_section.reshape(row_blocks, TILE)
    block_shape = (data_width, particles, TILE)
    slot = tile_slot.T
    design = pltpu.with_memory_space_constraint(design, pltpu.HBM)

    positions = pltpu.with_memory_space_constraint(positions, pltpu.HBM)
    chosen = pltpu.with_memory_space_constraint(block_choice, pltpu.HBM)
    outgoing, column = pl.pallas_call(
        select_kernel,
        out_shape=(
            jax.ShapeDtypeStruct(block_shape, bf16),
            jax.ShapeDtypeStruct((data_width,), jnp.int32),
        ),
        in_specs=[sspec(), hspec(), hspec()],
        out_specs=(vspec(), sspec()),
        scratch_shapes=[
            SMEM(block_choice.shape, jnp.int32),
            VMEM((particles, width), f32),
            VMEM((owned, particles, TILE), bf16),
            pltpu.SemaphoreType.DMA((2,)),
        ],
        compiler_params=params(4),
    )(me, chosen, positions)
    fetched = exchange(outgoing, "dp")
    terms = pl.pallas_call(
        gradient_kernel,
        out_shape=jax.ShapeDtypeStruct(block_shape, f32),
        in_specs=[sspec(), hspec(), vspec(), vspec(), vspec()],
        out_specs=vspec(),
        scratch_shapes=[VMEM(design.shape, bf16), pltpu.SemaphoreType.DMA((CHUNKS,))],
        compiler_params=params(12),
    )(slot, design, fetched, labels, sections)
    incoming = exchange(terms.astype(f16), "dp").astype(f32)
    moved, outgoing = pl.pallas_call(
        advance_kernel,
        out_shape=(
            jax.ShapeDtypeStruct((particles, width), f32),
            jax.ShapeDtypeStruct(block_shape, bf16),
        ),
        in_specs=[sspec(), hspec(), vspec()],
        out_specs=(vspec(), vspec()),
        scratch_shapes=[
            VMEM((particles, width), f32),
            VMEM((owned, particles, TILE), f32),
            VMEM((owned, particles, TILE), bf16),
            pltpu.SemaphoreType.DMA,
        ],
        compiler_params=params(6),
    )(column, positions, incoming)
    fetched_new = exchange(outgoing, "dp")
    everyone = [moved]
    for ahead in range(1, groups):
        ring = [(g, (g + ahead) % groups) for g in range(groups)]
        everyone.append(lax.ppermute(moved, "dom", ring))
    sums = pl.pallas_call(
        likelihood_kernel,
        out_shape=jax.ShapeDtypeStruct((data_width, 1, TILE), f32),
        in_specs=[sspec(), hspec(), vspec(), vspec(), vspec()],
        out_specs=vspec(),
        scratch_shapes=[VMEM(design.shape, bf16), pltpu.SemaphoreType.DMA((CHUNKS,))],
        compiler_params=params(12),
    )(slot, design, fetched_new, labels, sections)
    sums = exchange(sums, "dp")
    means = pl.pallas_call(
        functools.partial(mean_kernel, particles),
        out_shape=jax.ShapeDtypeStruct((groups, 1, TILE), f32),
        in_specs=[vspec()],
        out_specs=vspec(),
        compiler_params=params(1),
    )(sums)
    table = exchange(means, "dom")[:, 0]
    advanced = pl.pallas_call(
        pick_kernel,
        out_shape=jax.ShapeDtypeStruct((particles, width), f32),
        in_specs=[sspec(), sspec()] + [vspec()] * groups,
        out_specs=vspec(),
        scratch_shapes=[VMEM((groups * particles, width), f32), pltpu.SemaphoreType.DMA((groups,))],
        compiler_params=params(4),
    )(group, ancestors, *everyone)
    from_group = jnp.arange(groups)[None, :, None] == (ancestors // particles)[:, None, None]
    from_row = jnp.arange(TILE)[None, None, :] == (ancestors % particles)[:, None, None]
    means = jnp.sum(jnp.where(from_group & from_row, table[None], 0.0), axis=(1, 2))
    return advanced, means


def solution(mesh):
    return jax.shard_map(
        shards,
        mesh=mesh,
        in_specs=(P("dom", "dp"), P("dom"), P(), P("dp", None), P("dp", None), P("dp"), P("dp")),
        out_specs=(P("dom", "dp"), P("dom")),
        check_vma=False,
    )
```

time: 180 us -> 173 us (0.961)
  blocking collectives: 34.2 us -> 77 us
  waiting for transfers between devices: 54.7 us -> 26.6 us
  starting transfers between devices: 62.3 us -> 47.4 us
  local copies, waits for them, and re-layouts: 3.63 us -> 0.02 us
  Pallas kernels: 20.4 us -> 17.9 us
    all_to_all x1 -> x2, blocking collectives: 34.2 us -> 77 us  [exchange(): return lax.all_to_all(x, axes, split_axis=0, concat_axis=0, tiled=True)]
    all_to_all x4 -> x3, waiting for transfers between devices: 48.8 us -> 20.7 us  [exchange(): return lax.all_to_all(x, axes, split_axis=0, concat_axis=0, tiled=True)]
    all_to_all x4 -> x3, starting transfers between devices: 30.7 us -> 15.8 us  [exchange(): return lax.all_to_all(x, axes, split_axis=0, concat_axis=0, tiled=True)]
    pallas_call x1, Pallas kernels: 7.63 us -> 4.69 us  [shards(): pl.pallas_call(gradient_kernel, out_shape=jax.ShapeDtypeStruct(block_shap...]
    unnamed x17 -> x8, local copies, waits for them, and re-layouts: 2.45 us -> 0.02 us
  transfers between devices with their start and end apart: 11 -> 10, of which waited for: 4 -> 3; matrix products, arithmetic and copies ran while one was open for 1% -> 0% of each run, Pallas kernels for 4% -> 5%
where the time goes in v3:
time: 173 us; the launch traced here: 172 us
  blocking collectives  77 us (45%)
  starting transfers between devices  47.4 us (27%)
  waiting for transfers between devices  26.6 us (15%)
  Pallas kernels  17.9 us (10%)
  other arithmetic  2.06 us (1%)
    all_to_all x2, blocking collectives, exchange(): return lax.all_to_all(x, axes, split_axis=0, concat_axis=0, tiled=True)  77 us
    ppermute x7, starting transfers between devices, shards(): everyone.append(lax.ppermute(moved, 'dom', ring))  31.6 us
    all_to_all x3, waiting for transfers between devices, exchange(): return lax.all_to_all(x, axes, split_axis=0, concat_axis=0, tiled=True)  20.7 us
    all_to_all x3, starting transfers between devices, exchange(): return lax.all_to_all(x, axes, split_axis=0, concat_axis=0, tiled=True)  15.8 us
    ppermute x7, waiting for transfers between devices, shards(): everyone.append(lax.ppermute(moved, 'dom', ring))  5.86 us
    pallas_call x1, Pallas kernels, shards(): pl.pallas_call(gradient_kernel, out_shape=jax.ShapeDtypeStruct(block_shap...  4.69 us
    pallas_call x1, Pallas kernels, shards(): pl.pallas_call(likelihood_kernel, out_shape=jax.ShapeDtypeStruct((data_wi...  4.64 us
  transfers between devices with their start and end apart: 10, of which 3 were waited for; matrix products, arithmetic and copies ran while one was open for 0% of the time, Pallas kernels for 5%

profile of v3, /device:TPU:1, one launch (start us, length us, event | category | flops | bytes accessed | tf_op | source)
XLA Modules:
  0.0 171.9 jit_solution(2084985009111476975)
XLA Ops:
  0.7 2.1 %shard_map.86 = (bf16[64,64,128]{2,1,0:T(8,128)(2,1)S(1)}, s32[64]{0:T(128)S(1)}) custom-call(s32[1]{0:T(128)} %bitcast.1.me, s32[64,64]{1,0:T(8,128)} %choice.1, f32[64,512]{1,0:T(8,128)} %positions.3), custom_call_target="tpu_custom_call" | custom-call | tf_op jit(solution)/shard_map/pallas_call | solution.py:204
  2.8 42.8 %all_to_all.25.fetched = bf16[64,64,128]{2,1,0:T(8,128)(2,1)S(1)} all-to-all(bf16[64,64,128]{2,1,0:T(8,128)(2,1)S(1)} %get-tuple-element.7), channel_id=1, replica_groups=mesh['dom'=8,'dp'=64] {'dp'}, dimensions={0} | all-to-all | bytes 2097152 | tf_op jit(solution)/shard_map/all_to_all | solution.py:42
  45.6 4.7 %shard_map.87 = f32[64,64,128]{2,1,0:T(8,128)S(1)} custom-call(s32[8,16]{1,0:T(8,128)S(1)} %bitcast.10, bf16[2048,1024]{1,0:T(8,128)(2,1)} %design.3, bf16[64,64,128]{2,1,0:T(8,128)(2,1)S(1)} %all_to_all.25.fetched, s32[16,128]{1,0:T(8,128)S(1)} %bitcast.6, s32[16,128]{1,0:T(8,128)S(1)} %bitcast.8), custom_call_target="tpu_custom_call" | custom-call | tf_op jit(solution)/shard_map/pallas_call | solution.py:221
  50.3 0.2 convert_element_type.6
  50.6 34.2 %all_to_all.26 = f16[64,64,128]{2,1,0:T(8,128)(2,1)S(1)} all-to-all(f16[64,64,128]{2,1,0:T(8,128)(2,1)S(1)} %convert_element_type.6), channel_id=1, replica_groups=mesh['dom'=8,'dp'=64] {'dp'}, dimensions={0} | all-to-all | bytes 2097152 | tf_op jit(solution)/shard_map/all_to_all | solution.py:42
  84.8 0.2 convert_element_type.7.incoming
  85.0 2.6 %shard_map.88 = (f32[64,512]{1,0:T(8,128)S(1)}, bf16[64,64,128]{2,1,0:T(8,128)(2,1)}) custom-call(s32[64]{0:T(128)S(1)} %get-tuple-element.6.column, f32[64,512]{1,0:T(8,128)} %positions.3, f32[64,64,128]{2,1,0:T(8,128)S(1)} %convert_element_type.7.incoming), custom_call_target="tpu_custom_call" | custom-call | tf_op jit(solution)/shard_map/pallas_call | solution.py:230
  87.6 6.3 %all-to-all-start.2 = ((bf16[64,64,128]{2,1,0:T(8,128)(2,1)}), bf16[64,64,128]{2,1,0:T(8,128)(2,1)S(1)}, u32[]{:S(2)}, u32[]{:S(2)}) async-start(bf16[64,64,128]{2,1,0:T(8,128)(2,1)} %get-tuple-element.9), calls=%async_computation.2 | async-start | bytes 2097152 | tf_op jit(solution)/shard_map/all_to_all | solution.py:42
  93.9 3.2 %collective-permute-start = (f32[64,512]{1,0:T(8,128)S(1)}, f32[64,512]{1,0:T(8,128)S(1)}, u32[]{:S(2)}, u32[]{:S(2)}) collective-permute-start(f32[64,512]{1,0:T(8,128)S(1)} %get-tuple-element.8.refs_0_), channel_id=1, source_target_pairs={{0,64},{64,128},{128,192},{192,256},{256,320},{320,384},{384,448},... | collective-permute-start | bytes 393224 | tf_op jit(solution)/shard_map/ppermute | solution.py:250
  97.1 4.2 %collective-permute-start.1 = (f32[64,512]{1,0:T(8,128)S(1)}, f32[64,512]{1,0:T(8,128)S(1)}, u32[]{:S(2)}, u32[]{:S(2)}) collective-permute-start(f32[64,512]{1,0:T(8,128)S(1)} %get-tuple-element.8.refs_0_), channel_id=1, source_target_pairs={{0,128},{64,192},{128,256},{192,320},{256,384},{320,448},{384,0},{... | collective-permute-start | bytes 393224 | tf_op jit(solution)/shard_map/ppermute | solution.py:250
  101.3 20.7 %all-to-all-done.2.fetched = bf16[64,64,128]{2,1,0:T(8,128)(2,1)S(1)} async-done(((bf16[64,64,128]{2,1,0:T(8,128)(2,1)}), bf16[64,64,128]{2,1,0:T(8,128)(2,1)S(1)}, u32[]{:S(2)}, u32[]{:S(2)}) %all-to-all-start.2) | async-done | bytes 1048608 | tf_op jit(solution)/shard_map/all_to_all | solution.py:42
  122.0 4.6 %shard_map.90 = f32[64,1,128]{2,1,0:T(1,128)} custom-call(s32[8,16]{1,0:T(8,128)S(1)} %bitcast.11, bf16[2048,1024]{1,0:T(8,128)(2,1)} %design.3, bf16[64,64,128]{2,1,0:T(8,128)(2,1)S(1)} %all-to-all-done.2.fetched, s32[16,128]{1,0:T(8,128)S(1)} %bitcast.7, s32[16,128]{1,0:T(8,128)S(1)} %bitcast.9), custom_call_target="tpu_custom_call" | custom-call | tf_op jit(solution)/shard_map/pallas_call | solution.py:251
  126.7 6.3 %all-to-all-start.3 = ((f32[64,1,128]{2,1,0:T(1,128)}), f32[64,1,128]{2,1,0:T(1,128)S(1)}, u32[]{:S(2)}, u32[]{:S(2)}) async-start(f32[64,1,128]{2,1,0:T(1,128)} %shard_map.90), calls=%async_computation.3 | async-start | bytes 65536 | tf_op jit(solution)/shard_map/all_to_all | solution.py:42
  133.1 5.2 %collective-permute-start.2 = (f32[64,512]{1,0:T(8,128)S(1)}, f32[64,512]{1,0:T(8,128)S(1)}, u32[]{:S(2)}, u32[]{:S(2)}) collective-permute-start(f32[64,512]{1,0:T(8,128)S(1)} %get-tuple-element.8.refs_0_), channel_id=1, source_target_pairs={{0,192},{64,256},{128,320},{192,384},{256,448},{320,0},{384,64},{4... | collective-permute-start | bytes 393224 | tf_op jit(solution)/shard_map/ppermute | solution.py:250
  138.3 4.8 %collective-permute-start.3 = (f32[64,512]{1,0:T(8,128)S(1)}, f32[64,512]{1,0:T(8,128)S(1)}, u32[]{:S(2)}, u32[]{:S(2)}) collective-permute-start(f32[64,512]{1,0:T(8,128)S(1)} %get-tuple-element.8.refs_0_), channel_id=1, source_target_pairs={{0,256},{64,320},{128,384},{192,448},{256,0},{320,64},{384,128},{4... | collective-permute-start | bytes 393224 | tf_op jit(solution)/shard_map/ppermute | solution.py:250
  143.1 5.8 %collective-permute-start.4 = (f32[64,512]{1,0:T(8,128)S(1)}, f32[64,512]{1,0:T(8,128)S(1)}, u32[]{:S(2)}, u32[]{:S(2)}) collective-permute-start(f32[64,512]{1,0:T(8,128)S(1)} %get-tuple-element.8.refs_0_), channel_id=1, source_target_pairs={{0,320},{64,384},{128,448},{192,0},{256,64},{320,128},{384,192},{4... | collective-permute-start | bytes 393224 | tf_op jit(solution)/shard_map/ppermute | solution.py:250
  148.8 0.7 shard_map.91
  149.6 3.2 %all-to-all-start.4 = ((f32[8,1,128]{2,1,0:T(1,128)}), f32[8,1,128]{2,1,0:T(1,128)S(1)}, u32[]{:S(2)}, u32[]{:S(2)}) async-start(f32[8,1,128]{2,1,0:T(1,128)} %shard_map.91), calls=%async_computation.4 | async-start | bytes 8192 | tf_op jit(solution)/shard_map/all_to_all | solution.py:42
  152.8 5.4 %collective-permute-start.5 = (f32[64,512]{1,0:T(8,128)S(1)}, f32[64,512]{1,0:T(8,128)S(1)}, u32[]{:S(2)}, u32[]{:S(2)}) collective-permute-start(f32[64,512]{1,0:T(8,128)S(1)} %get-tuple-element.8.refs_0_), channel_id=1, source_target_pairs={{0,384},{64,448},{128,0},{192,64},{256,128},{320,192},{384,256},{4... | collective-permute-start | bytes 393224 | tf_op jit(solution)/shard_map/ppermute | solution.py:250
  158.2 3.1 %collective-permute-start.6 = (f32[64,512]{1,0:T(8,128)S(1)}, f32[64,512]{1,0:T(8,128)S(1)}, u32[]{:S(2)}, u32[]{:S(2)}) collective-permute-start(f32[64,512]{1,0:T(8,128)S(1)} %get-tuple-element.8.refs_0_), channel_id=1, source_target_pairs={{0,448},{64,0},{128,64},{192,128},{256,192},{320,256},{384,320},{4... | collective-permute-start | bytes 393224 | tf_op jit(solution)/shard_map/ppermute | solution.py:250
  161.4 3.7 %collective-permute-done.5.refs_6_ = f32[64,512]{1,0:T(8,128)S(1)} collective-permute-done((f32[64,512]{1,0:T(8,128)S(1)}, f32[64,512]{1,0:T(8,128)S(1)}, u32[]{:S(2)}, u32[]{:S(2)}) %collective-permute-start.5) | collective-permute-done | bytes 131104 | tf_op jit(solution)/shard_map/ppermute | solution.py:250
  165.2 2.1 %collective-permute-done.6.refs_7_ = f32[64,512]{1,0:T(8,128)S(1)} collective-permute-done((f32[64,512]{1,0:T(8,128)S(1)}, f32[64,512]{1,0:T(8,128)S(1)}, u32[]{:S(2)}, u32[]{:S(2)}) %collective-permute-start.6) | collective-permute-done | bytes 131104 | tf_op jit(solution)/shard_map/ppermute | solution.py:250
  167.3 3.2 %shard_map.89 = f32[64,512]{1,0:T(8,128)} custom-call(s32[1]{0:T(128)} %bitcast.group, s32[64]{0:T(128)S(1)} %copy-done.3, f32[64,512]{1,0:T(8,128)S(1)} %get-tuple-element.8.refs_0_, f32[64,512]{1,0:T(8,128)S(1)} %collective-permute-done.refs_1_, f32[64,512]{1,0:T(8,128)S(1)} %collective-permute-done.1.refs_2_, ...), custom_call_target="tpu_custom_call" | custom-call | tf_op jit(solution)/shard_map/pallas_call | solution.py:268
  170.5 1.5 select_reduce_fusion
  (18 shorter events, 0.2 us)
Async XLA Ops:
  0.6 45.0 %copy-start.2 = (s32[16,8]{0,1:T(8,128)S(1)}, s32[16,8]{0,1:T(8,128)}, u32[]{:S(2)}) copy-start(s32[16,8]{0,1:T(8,128)} %param.10) | copy-start | bytes 1540
  0.6 45.0 %copy-start = (s32[2048]{0:T(1024)S(1)}, s32[2048]{0:T(1024)}, u32[]{:S(2)}) copy-start(s32[2048]{0:T(1024)} %param.12) | copy-start | bytes 24580
  0.7 45.0 %copy-start.1 = (s32[2048]{0:T(1024)S(1)}, s32[2048]{0:T(1024)}, u32[]{:S(2)}) copy-start(s32[2048]{0:T(1024)} %param.13) | copy-start | bytes 24580
  85.0 8.9 %copy-start.3 = (s32[64]{0:T(128)S(1)}, s32[64]{0:T(128)}, u32[]{:S(2)}) copy-start(s32[64]{0:T(128)} %ancestors.1) | copy-start | bytes 772
  87.6 34.5 %all-to-all-start.2 = ((bf16[64,64,128]{2,1,0:T(8,128)(2,1)}), bf16[64,64,128]{2,1,0:T(8,128)(2,1)S(1)}, u32[]{:S(2)}, u32[]{:S(2)}) async-start(bf16[64,64,128]{2,1,0:T(8,128)(2,1)} %get-tuple-element.9), calls=%async_computation.2 | async-start | bytes 2097152 | tf_op jit(solution)/shard_map/all_to_all | solution.py:42
  93.9 58.9 %collective-permute-start = (f32[64,512]{1,0:T(8,128)S(1)}, f32[64,512]{1,0:T(8,128)S(1)}, u32[]{:S(2)}, u32[]{:S(2)}) collective-permute-start(f32[64,512]{1,0:T(8,128)S(1)} %get-tuple-element.8.refs_0_), channel_id=1, source_target_pairs={{0,64},{64,128},{128,192},{192,256},{256,320},{320,384},{384,448},... | collective-permute-start | bytes 393224 | tf_op jit(solution)/shard_map/ppermute | solution.py:250
  97.1 61.1 %collective-permute-start.1 = (f32[64,512]{1,0:T(8,128)S(1)}, f32[64,512]{1,0:T(8,128)S(1)}, u32[]{:S(2)}, u32[]{:S(2)}) collective-permute-start(f32[64,512]{1,0:T(8,128)S(1)} %get-tuple-element.8.refs_0_), channel_id=1, source_target_pairs={{0,128},{64,192},{128,256},{192,320},{256,384},{320,448},{384,0},{... | collective-permute-start | bytes 393224 | tf_op jit(solution)/shard_map/ppermute | solution.py:250
  126.7 22.1 %all-to-all-start.3 = ((f32[64,1,128]{2,1,0:T(1,128)}), f32[64,1,128]{2,1,0:T(1,128)S(1)}, u32[]{:S(2)}, u32[]{:S(2)}) async-start(f32[64,1,128]{2,1,0:T(1,128)} %shard_map.90), calls=%async_computation.3 | async-start | bytes 65536 | tf_op jit(solution)/shard_map/all_to_all | solution.py:42
  133.1 28.3 %collective-permute-start.2 = (f32[64,512]{1,0:T(8,128)S(1)}, f32[64,512]{1,0:T(8,128)S(1)}, u32[]{:S(2)}, u32[]{:S(2)}) collective-permute-start(f32[64,512]{1,0:T(8,128)S(1)} %get-tuple-element.8.refs_0_), channel_id=1, source_target_pairs={{0,192},{64,256},{128,320},{192,384},{256,448},{320,0},{384,64},{4... | collective-permute-start | bytes 393224 | tf_op jit(solution)/shard_map/ppermute | solution.py:250
  138.3 23.1 %collective-permute-start.3 = (f32[64,512]{1,0:T(8,128)S(1)}, f32[64,512]{1,0:T(8,128)S(1)}, u32[]{:S(2)}, u32[]{:S(2)}) collective-permute-start(f32[64,512]{1,0:T(8,128)S(1)} %get-tuple-element.8.refs_0_), channel_id=1, source_target_pairs={{0,256},{64,320},{128,384},{192,448},{256,0},{320,64},{384,128},{4... | collective-permute-start | bytes 393224 | tf_op jit(solution)/shard_map/ppermute | solution.py:250
  143.1 18.4 %collective-permute-start.4 = (f32[64,512]{1,0:T(8,128)S(1)}, f32[64,512]{1,0:T(8,128)S(1)}, u32[]{:S(2)}, u32[]{:S(2)}) collective-permute-start(f32[64,512]{1,0:T(8,128)S(1)} %get-tuple-element.8.refs_0_), channel_id=1, source_target_pairs={{0,320},{64,384},{128,448},{192,0},{256,64},{320,128},{384,192},{4... | collective-permute-start | bytes 393224 | tf_op jit(solution)/shard_map/ppermute | solution.py:250
  149.6 20.9 %all-to-all-start.4 = ((f32[8,1,128]{2,1,0:T(1,128)}), f32[8,1,128]{2,1,0:T(1,128)S(1)}, u32[]{:S(2)}, u32[]{:S(2)}) async-start(f32[8,1,128]{2,1,0:T(1,128)} %shard_map.91), calls=%async_computation.4 | async-start | bytes 8192 | tf_op jit(solution)/shard_map/all_to_all | solution.py:42
  152.8 12.3 %collective-permute-start.5 = (f32[64,512]{1,0:T(8,128)S(1)}, f32[64,512]{1,0:T(8,128)S(1)}, u32[]{:S(2)}, u32[]{:S(2)}) collective-permute-start(f32[64,512]{1,0:T(8,128)S(1)} %get-tuple-element.8.refs_0_), channel_id=1, source_target_pairs={{0,384},{64,448},{128,0},{192,64},{256,128},{320,192},{384,256},{4... | collective-permute-start | bytes 393224 | tf_op jit(solution)/shard_map/ppermute | solution.py:250
  158.2 9.0 %collective-permute-start.6 = (f32[64,512]{1,0:T(8,128)S(1)}, f32[64,512]{1,0:T(8,128)S(1)}, u32[]{:S(2)}, u32[]{:S(2)}) collective-permute-start(f32[64,512]{1,0:T(8,128)S(1)} %get-tuple-element.8.refs_0_), channel_id=1, source_target_pairs={{0,448},{64,0},{128,64},{192,128},{256,192},{320,256},{384,320},{4... | collective-permute-start | bytes 393224 | tf_op jit(solution)/shard_map/ppermute | solution.py:250

commit v4 on v3

--- a/solution.py
+++ b/solution.py
@@ -11,6 +11,7 @@
 TILE = 128
 CURRENT = 2
 CHUNKS = 4
+COST = 1 << 30
 step_size = 1.0
 prior_precision = 0.05
 
@@ -82,11 +83,8 @@
     ]
 
 
-def gradient_kernel(slot, design, fetched, labels, sections, outgoing, held, sems):
+def gradient_kernel(slot, held, fetched, labels, sections, outgoing):
     per_block, row_blocks = slot.shape
-    copies = chunk_copies(design, held, sems)
-    for copy in copies:
-        copy.start()
     outgoing[...] = jnp.zeros_like(outgoing)
 
     def tiles_of(b):
@@ -94,8 +92,6 @@
 
     residuals = []
     for b in range(row_blocks):
-        if b % (row_blocks // len(copies)) == 0:
-            copies[b // (row_blocks // len(copies))].wait()
         logits = logits_of(weights_of(slot, fetched, b, per_block), tiles_of(b))
         target = labels[b : b + 1, :].astype(f32)
         active = sections[b : b + 1, :] <= CURRENT
@@ -197,6 +193,7 @@
     sections = row_section.reshape(row_blocks, TILE)
     block_shape = (data_width, particles, TILE)
     slot = tile_slot.T
+    near = design
     design = pltpu.with_memory_space_constraint(design, pltpu.HBM)
 
     positions = pltpu.with_memory_space_constraint(positions, pltpu.HBM)
@@ -215,17 +212,17 @@
             VMEM((owned, particles, TILE), bf16),
             pltpu.SemaphoreType.DMA((2,)),
         ],
+        cost_estimate=pl.CostEstimate(flops=COST, bytes_accessed=COST, transcendentals=0),
         compiler_params=params(4),
     )(me, chosen, positions)
     fetched = exchange(outgoing, "dp")
     terms = pl.pallas_call(
         gradient_kernel,
         out_shape=jax.ShapeDtypeStruct(block_shape, f32),
-        in_specs=[sspec(), hspec(), vspec(), vspec(), vspec()],
-        out_specs=vspec(),
-        scratch_shapes=[VMEM(design.shape, bf16), pltpu.SemaphoreType.DMA((CHUNKS,))],
-        compiler_params=params(12),
-    )(slot, design, fetched, labels, sections)
+        in_specs=[sspec(), vspec(), vspec(), vspec(), vspec()],
+        out_specs=vspec(),
+        compiler_params=params(8),
+    )(slot, near, fetched, labels, sections)
     incoming = exchange(terms.astype(f16), "dp").astype(f32)
     moved, outgoing = pl.pallas_call(
         advance_kernel,

time: 173 us -> 172 us (level)
  no operation moved by 1% of the time
where the time goes in v4:
time: 172 us; the launch traced here: 171 us
  blocking collectives  77 us (45%)
  starting transfers between devices  47.5 us (28%)
  waiting for transfers between devices  26.6 us (15%)
  Pallas kernels  16.4 us (10%)
  other arithmetic  2.06 us (1%)
    all_to_all x2, blocking collectives, exchange(): return lax.all_to_all(x, axes, split_axis=0, concat_axis=0, tiled=True)  77 us
    ppermute x7, starting transfers between devices, shards(): everyone.append(lax.ppermute(moved, 'dom', ring))  31.6 us
    all_to_all x3, waiting for transfers between devices, exchange(): return lax.all_to_all(x, axes, split_axis=0, concat_axis=0, tiled=True)  20.7 us
    all_to_all x3, starting transfers between devices, exchange(): return lax.all_to_all(x, axes, split_axis=0, concat_axis=0, tiled=True)  15.9 us
    ppermute x7, waiting for transfers between devices, shards(): everyone.append(lax.ppermute(moved, 'dom', ring))  5.91 us
    pallas_call x1, Pallas kernels, shards(): pl.pallas_call(likelihood_kernel, out_shape=jax.ShapeDtypeStruct((data_wi...  4.64 us
  transfers between devices with their start and end apart: 10, of which 3 were waited for; matrix products, arithmetic and copies ran while one was open for 0% of the time, Pallas kernels for 5%

profile of v4, /device:TPU:1, one launch (start us, length us, event | category | flops | bytes accessed | tf_op | source)
XLA Modules:
  0.0 170.6 jit_solution(17372883580402317477)
XLA Ops:
  0.7 2.1 %shard_map.86 = (bf16[64,64,128]{2,1,0:T(8,128)(2,1)S(1)}, s32[64]{0:T(128)S(1)}) custom-call(s32[1]{0:T(128)} %bitcast.1.me, s32[64,64]{1,0:T(8,128)} %choice.1, f32[64,512]{1,0:T(8,128)} %positions.3), custom_call_target="tpu_custom_call" | custom-call | flops 1073741824 | bytes 1073741824 | tf_op jit(solution)/shard_map/pallas_call | solution.py:201
  2.8 42.8 %all_to_all.25.fetched = bf16[64,64,128]{2,1,0:T(8,128)(2,1)S(1)} all-to-all(bf16[64,64,128]{2,1,0:T(8,128)(2,1)S(1)} %get-tuple-element.7), channel_id=1, replica_groups=mesh['dom'=8,'dp'=64] {'dp'}, dimensions={0} | all-to-all | bytes 2097152 | tf_op jit(solution)/shard_map/all_to_all | solution.py:43
  45.6 3.2 %shard_map.87 = f32[64,64,128]{2,1,0:T(8,128)S(1)} custom-call(s32[8,16]{1,0:T(8,128)S(1)} %bitcast.10, bf16[2048,1024]{1,0:T(8,128)(2,1)S(1)} %copy-done, bf16[64,64,128]{2,1,0:T(8,128)(2,1)S(1)} %all_to_all.25.fetched, s32[16,128]{1,0:T(8,128)S(1)} %bitcast.6, s32[16,128]{1,0:T(8,128)S(1)} %bitcast.8), custom_call_target="tpu_custom_call" | custom-call | tf_op jit(solution)/shard_map/pallas_call | solution.py:219
  48.8 0.2 convert_element_type.6
  49.1 34.2 %all_to_all.26 = f16[64,64,128]{2,1,0:T(8,128)(2,1)S(1)} all-to-all(f16[64,64,128]{2,1,0:T(8,128)(2,1)S(1)} %convert_element_type.6), channel_id=1, replica_groups=mesh['dom'=8,'dp'=64] {'dp'}, dimensions={0} | all-to-all | bytes 2097152 | tf_op jit(solution)/shard_map/all_to_all | solution.py:43
  83.3 0.2 convert_element_type.7.incoming
  83.5 2.6 %shard_map.88 = (f32[64,512]{1,0:T(8,128)S(1)}, bf16[64,64,128]{2,1,0:T(8,128)(2,1)}) custom-call(s32[64]{0:T(128)S(1)} %get-tuple-element.6.column, f32[64,512]{1,0:T(8,128)} %positions.3, f32[64,64,128]{2,1,0:T(8,128)S(1)} %convert_element_type.7.incoming), custom_call_target="tpu_custom_call" | custom-call | tf_op jit(solution)/shard_map/pallas_call | solution.py:227
  86.1 6.3 %all-to-all-start.2 = ((bf16[64,64,128]{2,1,0:T(8,128)(2,1)}), bf16[64,64,128]{2,1,0:T(8,128)(2,1)S(1)}, u32[]{:S(2)}, u32[]{:S(2)}) async-start(bf16[64,64,128]{2,1,0:T(8,128)(2,1)} %get-tuple-element.9), calls=%async_computation.2 | async-start | bytes 2097152 | tf_op jit(solution)/shard_map/all_to_all | solution.py:43
  92.4 3.2 %collective-permute-start = (f32[64,512]{1,0:T(8,128)S(1)}, f32[64,512]{1,0:T(8,128)S(1)}, u32[]{:S(2)}, u32[]{:S(2)}) collective-permute-start(f32[64,512]{1,0:T(8,128)S(1)} %get-tuple-element.8.refs_0_), channel_id=1, source_target_pairs={{0,64},{64,128},{128,192},{192,256},{256,320},{320,384},{384,448},... | collective-permute-start | bytes 393224 | tf_op jit(solution)/shard_map/ppermute | solution.py:247
  95.6 4.2 %collective-permute-start.1 = (f32[64,512]{1,0:T(8,128)S(1)}, f32[64,512]{1,0:T(8,128)S(1)}, u32[]{:S(2)}, u32[]{:S(2)}) collective-permute-start(f32[64,512]{1,0:T(8,128)S(1)} %get-tuple-element.8.refs_0_), channel_id=1, source_target_pairs={{0,128},{64,192},{128,256},{192,320},{256,384},{320,448},{384,0},{... | collective-permute-start | bytes 393224 | tf_op jit(solution)/shard_map/ppermute | solution.py:247
  99.8 20.7 %all-to-all-done.2.fetched = bf16[64,64,128]{2,1,0:T(8,128)(2,1)S(1)} async-done(((bf16[64,64,128]{2,1,0:T(8,128)(2,1)}), bf16[64,64,128]{2,1,0:T(8,128)(2,1)S(1)}, u32[]{:S(2)}, u32[]{:S(2)}) %all-to-all-start.2) | async-done | bytes 1048608 | tf_op jit(solution)/shard_map/all_to_all | solution.py:43
  120.5 4.6 %shard_map.90 = f32[64,1,128]{2,1,0:T(1,128)} custom-call(s32[8,16]{1,0:T(8,128)S(1)} %bitcast.11, bf16[2048,1024]{1,0:T(8,128)(2,1)} %design.1, bf16[64,64,128]{2,1,0:T(8,128)(2,1)S(1)} %all-to-all-done.2.fetched, s32[16,128]{1,0:T(8,128)S(1)} %bitcast.7, s32[16,128]{1,0:T(8,128)S(1)} %bitcast.9), custom_call_target="tpu_custom_call" | custom-call | tf_op jit(solution)/shard_map/pallas_call | solution.py:248
  125.2 6.3 %all-to-all-start.3 = ((f32[64,1,128]{2,1,0:T(1,128)}), f32[64,1,128]{2,1,0:T(1,128)S(1)}, u32[]{:S(2)}, u32[]{:S(2)}) async-start(f32[64,1,128]{2,1,0:T(1,128)} %shard_map.90), calls=%async_computation.3 | async-start | bytes 65536 | tf_op jit(solution)/shard_map/all_to_all | solution.py:43
  131.6 5.2 %collective-permute-start.2 = (f32[64,512]{1,0:T(8,128)S(1)}, f32[64,512]{1,0:T(8,128)S(1)}, u32[]{:S(2)}, u32[]{:S(2)}) collective-permute-start(f32[64,512]{1,0:T(8,128)S(1)} %get-tuple-element.8.refs_0_), channel_id=1, source_target_pairs={{0,192},{64,256},{128,320},{192,384},{256,448},{320,0},{384,64},{4... | collective-permute-start | bytes 393224 | tf_op jit(solution)/shard_map/ppermute | solution.py:247
  136.8 4.8 %collective-permute-start.3 = (f32[64,512]{1,0:T(8,128)S(1)}, f32[64,512]{1,0:T(8,128)S(1)}, u32[]{:S(2)}, u32[]{:S(2)}) collective-permute-start(f32[64,512]{1,0:T(8,128)S(1)} %get-tuple-element.8.refs_0_), channel_id=1, source_target_pairs={{0,256},{64,320},{128,384},{192,448},{256,0},{320,64},{384,128},{4... | collective-permute-start | bytes 393224 | tf_op jit(solution)/shard_map/ppermute | solution.py:247
  141.6 5.8 %collective-permute-start.4 = (f32[64,512]{1,0:T(8,128)S(1)}, f32[64,512]{1,0:T(8,128)S(1)}, u32[]{:S(2)}, u32[]{:S(2)}) collective-permute-start(f32[64,512]{1,0:T(8,128)S(1)} %get-tuple-element.8.refs_0_), channel_id=1, source_target_pairs={{0,320},{64,384},{128,448},{192,0},{256,64},{320,128},{384,192},{4... | collective-permute-start | bytes 393224 | tf_op jit(solution)/shard_map/ppermute | solution.py:247
  147.3 0.7 shard_map.91
  148.1 3.3 %all-to-all-start.4 = ((f32[8,1,128]{2,1,0:T(1,128)}), f32[8,1,128]{2,1,0:T(1,128)S(1)}, u32[]{:S(2)}, u32[]{:S(2)}) async-start(f32[8,1,128]{2,1,0:T(1,128)} %shard_map.91), calls=%async_computation.4 | async-start | bytes 8192 | tf_op jit(solution)/shard_map/all_to_all | solution.py:43
  151.4 5.4 %collective-permute-start.5 = (f32[64,512]{1,0:T(8,128)S(1)}, f32[64,512]{1,0:T(8,128)S(1)}, u32[]{:S(2)}, u32[]{:S(2)}) collective-permute-start(f32[64,512]{1,0:T(8,128)S(1)} %get-tuple-element.8.refs_0_), channel_id=1, source_target_pairs={{0,384},{64,448},{128,0},{192,64},{256,128},{320,192},{384,256},{4... | collective-permute-start | bytes 393224 | tf_op jit(solution)/shard_map/ppermute | solution.py:247
  156.8 3.1 %collective-permute-start.6 = (f32[64,512]{1,0:T(8,128)S(1)}, f32[64,512]{1,0:T(8,128)S(1)}, u32[]{:S(2)}, u32[]{:S(2)}) collective-permute-start(f32[64,512]{1,0:T(8,128)S(1)} %get-tuple-element.8.refs_0_), channel_id=1, source_target_pairs={{0,448},{64,0},{128,64},{192,128},{256,192},{320,256},{384,320},{4... | collective-permute-start | bytes 393224 | tf_op jit(solution)/shard_map/ppermute | solution.py:247
  160.0 3.9 %collective-permute-done.5.refs_6_ = f32[64,512]{1,0:T(8,128)S(1)} collective-permute-done((f32[64,512]{1,0:T(8,128)S(1)}, f32[64,512]{1,0:T(8,128)S(1)}, u32[]{:S(2)}, u32[]{:S(2)}) %collective-permute-start.5) | collective-permute-done | bytes 131104 | tf_op jit(solution)/shard_map/ppermute | solution.py:247
  163.9 2.0 %collective-permute-done.6.refs_7_ = f32[64,512]{1,0:T(8,128)S(1)} collective-permute-done((f32[64,512]{1,0:T(8,128)S(1)}, f32[64,512]{1,0:T(8,128)S(1)}, u32[]{:S(2)}, u32[]{:S(2)}) %collective-permute-start.6) | collective-permute-done | bytes 131104 | tf_op jit(solution)/shard_map/ppermute | solution.py:247
  165.9 3.2 %shard_map.89 = f32[64,512]{1,0:T(8,128)} custom-call(s32[1]{0:T(128)} %bitcast.group, s32[64]{0:T(128)S(1)} %copy-done.4, f32[64,512]{1,0:T(8,128)S(1)} %get-tuple-element.8.refs_0_, f32[64,512]{1,0:T(8,128)S(1)} %collective-permute-done.refs_1_, f32[64,512]{1,0:T(8,128)S(1)} %collective-permute-done.1.refs_2_, ...), custom_call_target="tpu_custom_call" | custom-call | tf_op jit(solution)/shard_map/pallas_call | solution.py:265
  169.1 1.5 select_reduce_fusion
  (20 shorter events, 0.2 us)
Async XLA Ops:
  0.6 45.0 %copy-start = (bf16[2048,1024]{1,0:T(8,128)(2,1)S(1)}, bf16[2048,1024]{1,0:T(8,128)(2,1)}, u32[]{:S(2)}) copy-start(bf16[2048,1024]{1,0:T(8,128)(2,1)} %design.1) | copy-start | bytes 12582916
  0.6 45.0 %copy-start.1 = (s32[2048]{0:T(1024)S(1)}, s32[2048]{0:T(1024)}, u32[]{:S(2)}) copy-start(s32[2048]{0:T(1024)} %param.12) | copy-start | bytes 24580
  0.7 45.0 %copy-start.2 = (s32[2048]{0:T(1024)S(1)}, s32[2048]{0:T(1024)}, u32[]{:S(2)}) copy-start(s32[2048]{0:T(1024)} %param.13) | copy-start | bytes 24580
  0.7 45.0 %copy-start.3 = (s32[16,8]{0,1:T(8,128)S(1)}, s32[16,8]{0,1:T(8,128)}, u32[]{:S(2)}) copy-start(s32[16,8]{0,1:T(8,128)} %param.10) | copy-start | bytes 1540
  83.5 8.9 %copy-start.4 = (s32[64]{0:T(128)S(1)}, s32[64]{0:T(128)}, u32[]{:S(2)}) copy-start(s32[64]{0:T(128)} %ancestors.1) | copy-start | bytes 772
  86.1 34.5 %all-to-all-start.2 = ((bf16[64,64,128]{2,1,0:T(8,128)(2,1)}), bf16[64,64,128]{2,1,0:T(8,128)(2,1)S(1)}, u32[]{:S(2)}, u32[]{:S(2)}) async-start(bf16[64,64,128]{2,1,0:T(8,128)(2,1)} %get-tuple-element.9), calls=%async_computation.2 | async-start | bytes 2097152 | tf_op jit(solution)/shard_map/all_to_all | solution.py:43
  92.4 59.0 %collective-permute-start = (f32[64,512]{1,0:T(8,128)S(1)}, f32[64,512]{1,0:T(8,128)S(1)}, u32[]{:S(2)}, u32[]{:S(2)}) collective-permute-start(f32[64,512]{1,0:T(8,128)S(1)} %get-tuple-element.8.refs_0_), channel_id=1, source_target_pairs={{0,64},{64,128},{128,192},{192,256},{256,320},{320,384},{384,448},... | collective-permute-start | bytes 393224 | tf_op jit(solution)/shard_map/ppermute | solution.py:247
  95.6 61.2 %collective-permute-start.1 = (f32[64,512]{1,0:T(8,128)S(1)}, f32[64,512]{1,0:T(8,128)S(1)}, u32[]{:S(2)}, u32[]{:S(2)}) collective-permute-start(f32[64,512]{1,0:T(8,128)S(1)} %get-tuple-element.8.refs_0_), channel_id=1, source_target_pairs={{0,128},{64,192},{128,256},{192,320},{256,384},{320,448},{384,0},{... | collective-permute-start | bytes 393224 | tf_op jit(solution)/shard_map/ppermute | solution.py:247
  125.2 22.1 %all-to-all-start.3 = ((f32[64,1,128]{2,1,0:T(1,128)}), f32[64,1,128]{2,1,0:T(1,128)S(1)}, u32[]{:S(2)}, u32[]{:S(2)}) async-start(f32[64,1,128]{2,1,0:T(1,128)} %shard_map.90), calls=%async_computation.3 | async-start | bytes 65536 | tf_op jit(solution)/shard_map/all_to_all | solution.py:43
  131.6 28.4 %collective-permute-start.2 = (f32[64,512]{1,0:T(8,128)S(1)}, f32[64,512]{1,0:T(8,128)S(1)}, u32[]{:S(2)}, u32[]{:S(2)}) collective-permute-start(f32[64,512]{1,0:T(8,128)S(1)} %get-tuple-element.8.refs_0_), channel_id=1, source_target_pairs={{0,192},{64,256},{128,320},{192,384},{256,448},{320,0},{384,64},{4... | collective-permute-start | bytes 393224 | tf_op jit(solution)/shard_map/ppermute | solution.py:247
  136.8 23.2 %collective-permute-start.3 = (f32[64,512]{1,0:T(8,128)S(1)}, f32[64,512]{1,0:T(8,128)S(1)}, u32[]{:S(2)}, u32[]{:S(2)}) collective-permute-start(f32[64,512]{1,0:T(8,128)S(1)} %get-tuple-element.8.refs_0_), channel_id=1, source_target_pairs={{0,256},{64,320},{128,384},{192,448},{256,0},{320,64},{384,128},{4... | collective-permute-start | bytes 393224 | tf_op jit(solution)/shard_map/ppermute | solution.py:247
  141.6 18.5 %collective-permute-start.4 = (f32[64,512]{1,0:T(8,128)S(1)}, f32[64,512]{1,0:T(8,128)S(1)}, u32[]{:S(2)}, u32[]{:S(2)}) collective-permute-start(f32[64,512]{1,0:T(8,128)S(1)} %get-tuple-element.8.refs_0_), channel_id=1, source_target_pairs={{0,320},{64,384},{128,448},{192,0},{256,64},{320,128},{384,192},{4... | collective-permute-start | bytes 393224 | tf_op jit(solution)/shard_map/ppermute | solution.py:247
  148.1 21.0 %all-to-all-start.4 = ((f32[8,1,128]{2,1,0:T(1,128)}), f32[8,1,128]{2,1,0:T(1,128)S(1)}, u32[]{:S(2)}, u32[]{:S(2)}) async-start(f32[8,1,128]{2,1,0:T(1,128)} %shard_map.91), calls=%async_computation.4 | async-start | bytes 8192 | tf_op jit(solution)/shard_map/all_to_all | solution.py:43
  151.4 12.5 %collective-permute-start.5 = (f32[64,512]{1,0:T(8,128)S(1)}, f32[64,512]{1,0:T(8,128)S(1)}, u32[]{:S(2)}, u32[]{:S(2)}) collective-permute-start(f32[64,512]{1,0:T(8,128)S(1)} %get-tuple-element.8.refs_0_), channel_id=1, source_target_pairs={{0,384},{64,448},{128,0},{192,64},{256,128},{320,192},{384,256},{4... | collective-permute-start | bytes 393224 | tf_op jit(solution)/shard_map/ppermute | solution.py:247
  156.8 9.1 %collective-permute-start.6 = (f32[64,512]{1,0:T(8,128)S(1)}, f32[64,512]{1,0:T(8,128)S(1)}, u32[]{:S(2)}, u32[]{:S(2)}) collective-permute-start(f32[64,512]{1,0:T(8,128)S(1)} %get-tuple-element.8.refs_0_), channel_id=1, source_target_pairs={{0,448},{64,0},{128,64},{192,128},{256,192},{320,256},{384,320},{4... | collective-permute-start | bytes 393224 | tf_op jit(solution)/shard_map/ppermute | solution.py:247

commit v5 on v4

--- a/solution.py
+++ b/solution.py
@@ -129,13 +129,17 @@
     lax.fori_loop(0, outgoing.shape[0], send, 0, unroll=8)
 
 
-def pick_kernel(group, ancestors, *refs):
+def pick_kernel(places, group, ancestors, *refs):
     moved, (resampled, table, sems) = refs[:-3], refs[-3:]
     particles = resampled.shape[0]
-    groups = len(moved)
+    groups = len(places)
     copies = [
-        pltpu.make_async_copy(moved[k], table.at[pl.ds(k * particles, particles)], sems.at[k])
-        for k in range(groups)
+        pltpu.make_async_copy(
+            moved[which].at[pl.ds(part * particles, particles)],
+            table.at[pl.ds(ahead * particles, particles)],
+            sems.at[ahead],
+        )
+        for ahead, (which, part) in enumerate(places)
     ]
     for copy in copies:
         copy.start()
@@ -241,10 +245,18 @@
         compiler_params=params(6),
     )(column, positions, incoming)
     fetched_new = exchange(outgoing, "dp")
-    everyone = [moved]
-    for ahead in range(1, groups):
-        ring = [(g, (g + ahead) % groups) for g in range(groups)]
-        everyone.append(lax.ppermute(moved, "dom", ring))
+
+    def turn(x, ahead):
+        return lax.ppermute(x, "dom", [(g, (g + ahead) % groups) for g in range(groups)])
+
+    assert groups == 8
+    below = turn(moved, 1)
+    above = turn(moved, 7)
+    three = jnp.concatenate([moved, below, above], axis=0)
+    further = turn(three, 3)
+    back = turn(three, 6)
+    everyone = [moved, below, above, further, back]
+    places = [(0, 0), (1, 0), (3, 2), (3, 0), (3, 1), (4, 2), (4, 0), (2, 0)]
     sums = pl.pallas_call(
         likelihood_kernel,
         out_shape=jax.ShapeDtypeStruct((data_width, 1, TILE), f32),
@@ -263,9 +275,9 @@
     )(sums)
     table = exchange(means, "dom")[:, 0]
     advanced = pl.pallas_call(
-        pick_kernel,
+        functools.partial(pick_kernel, places),
         out_shape=jax.ShapeDtypeStruct((particles, width), f32),
-        in_specs=[sspec(), sspec()] + [vspec()] * groups,
+        in_specs=[sspec(), sspec()] + [vspec()] * len(everyone),
         out_specs=vspec(),
         scratch_shapes=[VMEM((groups * particles, width), f32), pltpu.SemaphoreType.DMA((groups,))],
         compiler_params=params(4),

time: 172 us -> 157 us (0.913)
  starting transfers between devices: 47.5 us -> 36 us
  waiting for transfers between devices: 26.6 us -> 24 us
    ppermute x7 -> x4, starting transfers between devices: 31.6 us -> 16.6 us  [turn(): lax.ppermute(x, 'dom', [(g, (g + ahead) % groups) for g in range(groups)])]
    ppermute x7 -> x4, waiting for transfers between devices: 5.91 us -> 2.37 us  [turn(): lax.ppermute(x, 'dom', [(g, (g + ahead) % groups) for g in range(groups)])]
    all_to_all x3, starting transfers between devices: 15.9 us -> 19.4 us  [exchange(): return lax.all_to_all(x, axes, split_axis=0, concat_axis=0, tiled=True)]
  transfers between devices with their start and end apart: 10 -> 7, of which waited for: 3 -> 5; matrix products, arithmetic and copies ran while one was open for 0% -> 0% of each run, Pallas kernels for 5% -> 5%
where the time goes in v5:
time: 157 us; the launch traced here: 156 us
  blocking collectives  77 us (49%)
  starting transfers between devices  36 us (23%)
  waiting for transfers between devices  24 us (15%)
  Pallas kernels  16.4 us (10%)
  other arithmetic  2.06 us (1%)
    all_to_all x2, blocking collectives, exchange(): return lax.all_to_all(x, axes, split_axis=0, concat_axis=0, tiled=True)  77 us
    all_to_all x3, waiting for transfers between devices, exchange(): return lax.all_to_all(x, axes, split_axis=0, concat_axis=0, tiled=True)  21.6 us
    all_to_all x3, starting transfers between devices, exchange(): return lax.all_to_all(x, axes, split_axis=0, concat_axis=0, tiled=True)  19.4 us
    ppermute x4, starting transfers between devices, turn(): lax.ppermute(x, 'dom', [(g, (g + ahead) % groups) for g in range(groups)])  16.6 us
    pallas_call x1, Pallas kernels, shards(): pl.pallas_call(likelihood_kernel, out_shape=jax.ShapeDtypeStruct((data_wi...  4.64 us
    pallas_call x1, Pallas kernels, shards(): pl.pallas_call(functools.partial(pick_kernel, places), out_shape=jax.Shap...  3.19 us
    pallas_call x1, Pallas kernels, shards(): pl.pallas_call(gradient_kernel, out_shape=jax.ShapeDtypeStruct(block_shap...  3.18 us
  transfers between devices with their start and end apart: 7, of which 5 were waited for; matrix products, arithmetic and copies ran while one was open for 0% of the time, Pallas kernels for 5%

profile of v5, /device:TPU:1, one launch (start us, length us, event | category | flops | bytes accessed | tf_op | source)
XLA Modules:
  0.0 156.4 jit_solution(8025617912790943627)
XLA Ops:
  0.7 2.1 %shard_map.86 = (bf16[64,64,128]{2,1,0:T(8,128)(2,1)S(1)}, s32[64]{0:T(128)S(1)}) custom-call(s32[1]{0:T(128)} %bitcast.1.me, s32[64,64]{1,0:T(8,128)} %choice.1, f32[64,512]{1,0:T(8,128)} %positions.3), custom_call_target="tpu_custom_call" | custom-call | flops 1073741824 | bytes 1073741824 | tf_op jit(solution)/shard_map/pallas_call | solution.py:205
  2.8 42.8 %all_to_all.25.fetched = bf16[64,64,128]{2,1,0:T(8,128)(2,1)S(1)} all-to-all(bf16[64,64,128]{2,1,0:T(8,128)(2,1)S(1)} %get-tuple-element.7), channel_id=1, replica_groups=mesh['dom'=8,'dp'=64] {'dp'}, dimensions={0} | all-to-all | bytes 2097152 | tf_op jit(solution)/shard_map/all_to_all | solution.py:43
  45.6 3.2 %shard_map.87 = f32[64,64,128]{2,1,0:T(8,128)S(1)} custom-call(s32[8,16]{1,0:T(8,128)S(1)} %bitcast.10, bf16[2048,1024]{1,0:T(8,128)(2,1)S(1)} %copy-done, bf16[64,64,128]{2,1,0:T(8,128)(2,1)S(1)} %all_to_all.25.fetched, s32[16,128]{1,0:T(8,128)S(1)} %bitcast.6, s32[16,128]{1,0:T(8,128)S(1)} %bitcast.8), custom_call_target="tpu_custom_call" | custom-call | tf_op jit(solution)/shard_map/pallas_call | solution.py:223
  48.8 0.2 convert_element_type.6
  49.1 34.2 %all_to_all.26 = f16[64,64,128]{2,1,0:T(8,128)(2,1)S(1)} all-to-all(f16[64,64,128]{2,1,0:T(8,128)(2,1)S(1)} %convert_element_type.6), channel_id=1, replica_groups=mesh['dom'=8,'dp'=64] {'dp'}, dimensions={0} | all-to-all | bytes 2097152 | tf_op jit(solution)/shard_map/all_to_all | solution.py:43
  83.3 0.2 convert_element_type.7.incoming
  83.5 2.6 %shard_map.88 = (f32[64,512]{1,0:T(8,128)S(1)}, bf16[64,64,128]{2,1,0:T(8,128)(2,1)}) custom-call(s32[64]{0:T(128)S(1)} %get-tuple-element.6.column, f32[64,512]{1,0:T(8,128)} %positions.3, f32[64,64,128]{2,1,0:T(8,128)S(1)} %convert_element_type.7.incoming), custom_call_target="tpu_custom_call" | custom-call | tf_op jit(solution)/shard_map/pallas_call | solution.py:231
  86.1 6.3 %all-to-all-start.2 = ((bf16[64,64,128]{2,1,0:T(8,128)(2,1)}), bf16[64,64,128]{2,1,0:T(8,128)(2,1)S(1)}, u32[]{:S(2)}, u32[]{:S(2)}) async-start(bf16[64,64,128]{2,1,0:T(8,128)(2,1)} %get-tuple-element.9), calls=%async_computation.2 | async-start | bytes 2097152 | tf_op jit(solution)/shard_map/all_to_all | solution.py:43
  92.4 3.2 %collective-permute-start = (f32[64,512]{1,0:T(8,128)S(1)}, f32[64,512]{1,0:T(8,128)S(1)}, u32[]{:S(2)}, u32[]{:S(2)}) collective-permute-start(f32[64,512]{1,0:T(8,128)S(1)} %get-tuple-element.8.refs_0_), channel_id=1, source_target_pairs={{0,64},{64,128},{128,192},{192,256},{256,320},{320,384},{384,448},... | collective-permute-start | bytes 393224 | tf_op jit(solution)/shard_map/ppermute | solution.py:250
  95.6 3.8 %collective-permute-start.1 = (f32[64,512]{1,0:T(8,128)S(1)}, f32[64,512]{1,0:T(8,128)S(1)}, u32[]{:S(2)}, u32[]{:S(2)}) collective-permute-start(f32[64,512]{1,0:T(8,128)S(1)} %get-tuple-element.8.refs_0_), channel_id=1, source_target_pairs={{0,448},{64,0},{128,64},{192,128},{256,192},{320,256},{384,320},{4... | collective-permute-start | bytes 393224 | tf_op jit(solution)/shard_map/ppermute | solution.py:250
  99.5 1.4 collective-permute-done.refs_1_
  100.9 0.9 collective-permute-done.1.refs_2_
  101.8 7.6 %collective-permute-start.2 = (f32[192,512]{1,0:T(8,128)S(1)}, f32[192,512]{1,0:T(8,128)S(1)}, u32[]{:S(2)}, u32[]{:S(2)}) collective-permute-start(f32[192,512]{1,0:T(8,128)S(1)} %constant_dynamic-update-slice_fusion), channel_id=1, source_target_pairs={{0,192},{64,256},{128,320},{192,384},{256,448},{320,0},{384,64},{4... | collective-permute-start | bytes 1179656 | tf_op jit(solution)/shard_map/ppermute | solution.py:250
  109.5 1.9 %collective-permute-start.3 = (f32[192,512]{1,0:T(8,128)S(1)}, f32[192,512]{1,0:T(8,128)S(1)}, u32[]{:S(2)}, u32[]{:S(2)}) collective-permute-start(f32[192,512]{1,0:T(8,128)S(1)} %constant_dynamic-update-slice_fusion), channel_id=1, source_target_pairs={{0,384},{64,448},{128,0},{192,64},{256,128},{320,192},{384,256},{4... | collective-permute-start | bytes 1179656 | tf_op jit(solution)/shard_map/ppermute | solution.py:250
  111.4 9.1 %all-to-all-done.2.fetched = bf16[64,64,128]{2,1,0:T(8,128)(2,1)S(1)} async-done(((bf16[64,64,128]{2,1,0:T(8,128)(2,1)}), bf16[64,64,128]{2,1,0:T(8,128)(2,1)S(1)}, u32[]{:S(2)}, u32[]{:S(2)}) %all-to-all-start.2) | async-done | bytes 1048608 | tf_op jit(solution)/shard_map/all_to_all | solution.py:43
  120.5 4.6 %shard_map.90 = f32[64,1,128]{2,1,0:T(1,128)} custom-call(s32[8,16]{1,0:T(8,128)S(1)} %bitcast.11, bf16[2048,1024]{1,0:T(8,128)(2,1)} %design.1, bf16[64,64,128]{2,1,0:T(8,128)(2,1)S(1)} %all-to-all-done.2.fetched, s32[16,128]{1,0:T(8,128)S(1)} %bitcast.7, s32[16,128]{1,0:T(8,128)S(1)} %bitcast.9), custom_call_target="tpu_custom_call" | custom-call | tf_op jit(solution)/shard_map/pallas_call | solution.py:260
  125.2 6.3 %all-to-all-start.3 = ((f32[64,1,128]{2,1,0:T(1,128)}), f32[64,1,128]{2,1,0:T(1,128)S(1)}, u32[]{:S(2)}, u32[]{:S(2)}) async-start(f32[64,1,128]{2,1,0:T(1,128)} %shard_map.90), calls=%async_computation.3 | async-start | bytes 65536 | tf_op jit(solution)/shard_map/all_to_all | solution.py:43
  131.5 0.1 iota_compare_fusion
  131.6 9.3 %all-to-all-done.3.sums = f32[64,1,128]{2,1,0:T(1,128)S(1)} async-done(((f32[64,1,128]{2,1,0:T(1,128)}), f32[64,1,128]{2,1,0:T(1,128)S(1)}, u32[]{:S(2)}, u32[]{:S(2)}) %all-to-all-start.3) | async-done | bytes 32800 | tf_op jit(solution)/shard_map/all_to_all | solution.py:43
  140.8 0.7 shard_map.91
  141.6 6.8 %all-to-all-start.4 = ((f32[8,1,128]{2,1,0:T(1,128)}), f32[8,1,128]{2,1,0:T(1,128)S(1)}, u32[]{:S(2)}, u32[]{:S(2)}) async-start(f32[8,1,128]{2,1,0:T(1,128)} %shard_map.91), calls=%async_computation.4 | async-start | bytes 8192 | tf_op jit(solution)/shard_map/all_to_all | solution.py:43
  148.5 3.2 %shard_map.89 = f32[64,512]{1,0:T(8,128)} custom-call(s32[1]{0:T(128)} %bitcast.group, s32[64]{0:T(128)S(1)} %copy-done.4, f32[64,512]{1,0:T(8,128)S(1)} %get-tuple-element.8.refs_0_, f32[64,512]{1,0:T(8,128)S(1)} %collective-permute-done.refs_1_, f32[64,512]{1,0:T(8,128)S(1)} %collective-permute-done.1.refs_2_, ...), custom_call_target="tpu_custom_call" | custom-call | tf_op jit(solution)/shard_map/pallas_call | solution.py:277
  151.7 3.3 %all-to-all-done.4 = f32[8,1,128]{2,1,0:T(1,128)S(1)} async-done(((f32[8,1,128]{2,1,0:T(1,128)}), f32[8,1,128]{2,1,0:T(1,128)S(1)}, u32[]{:S(2)}, u32[]{:S(2)}) %all-to-all-start.4) | async-done | bytes 4128 | tf_op jit(solution)/shard_map/all_to_all | solution.py:43
  154.9 1.5 select_reduce_fusion
  (17 shorter events, 0.1 us)
Async XLA Ops:
  0.6 45.0 %copy-start = (bf16[2048,1024]{1,0:T(8,128)(2,1)S(1)}, bf16[2048,1024]{1,0:T(8,128)(2,1)}, u32[]{:S(2)}) copy-start(bf16[2048,1024]{1,0:T(8,128)(2,1)} %design.1) | copy-start | bytes 12582916
  0.6 45.0 %copy-start.1 = (s32[2048]{0:T(1024)S(1)}, s32[2048]{0:T(1024)}, u32[]{:S(2)}) copy-start(s32[2048]{0:T(1024)} %param.12) | copy-start | bytes 24580
  0.7 45.0 %copy-start.2 = (s32[2048]{0:T(1024)S(1)}, s32[2048]{0:T(1024)}, u32[]{:S(2)}) copy-start(s32[2048]{0:T(1024)} %param.13) | copy-start | bytes 24580
  0.7 45.0 %copy-start.3 = (s32[16,8]{0,1:T(8,128)S(1)}, s32[16,8]{0,1:T(8,128)}, u32[]{:S(2)}) copy-start(s32[16,8]{0,1:T(8,128)} %param.10) | copy-start | bytes 1540
  83.5 12.1 %copy-start.4 = (s32[64]{0:T(128)S(1)}, s32[64]{0:T(128)}, u32[]{:S(2)}) copy-start(s32[64]{0:T(128)} %ancestors.1) | copy-start | bytes 772
  86.1 34.5 %all-to-all-start.2 = ((bf16[64,64,128]{2,1,0:T(8,128)(2,1)}), bf16[64,64,128]{2,1,0:T(8,128)(2,1)S(1)}, u32[]{:S(2)}, u32[]{:S(2)}) async-start(bf16[64,64,128]{2,1,0:T(8,128)(2,1)} %get-tuple-element.9), calls=%async_computation.2 | async-start | bytes 2097152 | tf_op jit(solution)/shard_map/all_to_all | solution.py:43
  92.4 8.5 %collective-permute-start = (f32[64,512]{1,0:T(8,128)S(1)}, f32[64,512]{1,0:T(8,128)S(1)}, u32[]{:S(2)}, u32[]{:S(2)}) collective-permute-start(f32[64,512]{1,0:T(8,128)S(1)} %get-tuple-element.8.refs_0_), channel_id=1, source_target_pairs={{0,64},{64,128},{128,192},{192,256},{256,320},{320,384},{384,448},... | collective-permute-start | bytes 393224 | tf_op jit(solution)/shard_map/ppermute | solution.py:250
  95.6 6.2 %collective-permute-start.1 = (f32[64,512]{1,0:T(8,128)S(1)}, f32[64,512]{1,0:T(8,128)S(1)}, u32[]{:S(2)}, u32[]{:S(2)}) collective-permute-start(f32[64,512]{1,0:T(8,128)S(1)} %get-tuple-element.8.refs_0_), channel_id=1, source_target_pairs={{0,448},{64,0},{128,64},{192,128},{256,192},{320,256},{384,320},{4... | collective-permute-start | bytes 393224 | tf_op jit(solution)/shard_map/ppermute | solution.py:250
  101.8 46.6 %collective-permute-start.2 = (f32[192,512]{1,0:T(8,128)S(1)}, f32[192,512]{1,0:T(8,128)S(1)}, u32[]{:S(2)}, u32[]{:S(2)}) collective-permute-start(f32[192,512]{1,0:T(8,128)S(1)} %constant_dynamic-update-slice_fusion), channel_id=1, source_target_pairs={{0,192},{64,256},{128,320},{192,384},{256,448},{320,0},{384,64},{4... | collective-permute-start | bytes 1179656 | tf_op jit(solution)/shard_map/ppermute | solution.py:250
  109.5 39.0 %collective-permute-start.3 = (f32[192,512]{1,0:T(8,128)S(1)}, f32[192,512]{1,0:T(8,128)S(1)}, u32[]{:S(2)}, u32[]{:S(2)}) collective-permute-start(f32[192,512]{1,0:T(8,128)S(1)} %constant_dynamic-update-slice_fusion), channel_id=1, source_target_pairs={{0,384},{64,448},{128,0},{192,64},{256,128},{320,192},{384,256},{4... | collective-permute-start | bytes 1179656 | tf_op jit(solution)/shard_map/ppermute | solution.py:250
  125.2 15.6 %all-to-all-start.3 = ((f32[64,1,128]{2,1,0:T(1,128)}), f32[64,1,128]{2,1,0:T(1,128)S(1)}, u32[]{:S(2)}, u32[]{:S(2)}) async-start(f32[64,1,128]{2,1,0:T(1,128)} %shard_map.90), calls=%async_computation.3 | async-start | bytes 65536 | tf_op jit(solution)/shard_map/all_to_all | solution.py:43
  141.6 13.4 %all-to-all-start.4 = ((f32[8,1,128]{2,1,0:T(1,128)}), f32[8,1,128]{2,1,0:T(1,128)S(1)}, u32[]{:S(2)}, u32[]{:S(2)}) async-start(f32[8,1,128]{2,1,0:T(1,128)} %shard_map.91), calls=%async_computation.4 | async-start | bytes 8192 | tf_op jit(solution)/shard_map/all_to_all | solution.py:43
